TPU v7x, 32 devices: a whole 2x2x4 slice. The times are simulated.
32 devices in a mesh: donor: 16 (over z, y, x), gene: 2 (over core).
Axes of the slice: x: 2, y: 2, z: 4, core: 2. Of those that a mesh axis runs over, the one named last changes fastest.
Arguments:
- embeddings: bfloat16 [32768, 512], P('donor', 'gene')
- targets_by_gene: bfloat16 [5120, 32768], P(('gene', 'donor')), may hold values from -6 to 6
- cell_counts: int32 [16], P('donor'), may hold values from 1024 to 2048, as said below
Outputs:
- coefficients: float32 [512, 5120], P('donor', 'gene')
Inputs may be any that keep to these rules, and one draw needn't show every extreme that they name: `cell_counts`: every entry is a multiple of 128; some entry equals 2048 and some entry equals 2048/2.
All inputs are finite; a program needn't handle non-finite values.
Results may differ from a plain program's by a relative error of at most 0.0003.
Values may be sent and summed in bfloat16 or wider, within the bound.
No kernel may reach another device: no remote copies, remote signals or barrier semaphores. Data moves between devices by JAX's collectives and lax.ppermute only.
A program may use at most 128 MiB of HBM per device.

v0:
```python
import math

import jax
import jax.numpy as jnp
from jax import lax
from jax.sharding import PartitionSpec as P


def solve_both(lower_factor, right_cols):
    halfway = lax.linalg.triangular_solve(lower_factor, right_cols, left_side=True, lower=True)
    return lax.linalg.triangular_solve(
        lower_factor, halfway, left_side=True, lower=True, transpose_a=True
    )


def shards(embeddings, targets_by_gene, cell_counts):
    valid_count = cell_counts[0]
    gathered = lax.all_gather(embeddings, "gene", axis=1, tiled=True)
    row_total = gathered.shape[0]
    width = gathered.shape[1]
    donors = lax.axis_size("donor")
    row_valid = lax.broadcasted_iota(jnp.int32, (row_total, 1), 0) < valid_count
    masked = jnp.where(row_valid, gathered, jnp.zeros_like(gathered))
    gram_matrix = lax.dot_general(
        masked, masked, (((0,), (0,)), ((), ())), preferred_element_type=jnp.float32
    )
    by_rows = lax.all_to_all(targets_by_gene, "donor", split_axis=1, concat_axis=0, tiled=True)
    gram_matrix = lax.psum(gram_matrix, "donor")
    lower_factor = jnp.linalg.cholesky(gram_matrix)
    scale_total = math.sqrt(row_total * donors)
    cross_local = jnp.dot(by_rows, masked, preferred_element_type=jnp.float32)
    cross_sum = lax.psum(cross_local, "donor")
    scaled = scale_total * solve_both(lower_factor, cross_sum.T)
    share = width // donors
    first_row = lax.axis_index("donor") * share
    return lax.dynamic_slice_in_dim(scaled, first_row, share, 0)


def solution(mesh):
    placed = (P("donor", "gene"), P(("gene", "donor"), None), P("donor"))
    return jax.shard_map(
        shards, mesh=mesh, in_specs=placed, out_specs=P("donor", "gene"), check_vma=False
    )
```

profile of v0, /device:TPU:0, one launch (start us, length us, event | category | flops | bytes accessed | tf_op | source)
XLA Modules:
  0.0 653.4 jit_solution(13016904788041452031)
XLA Ops:
  6.5 10.0 %copy.17 = bf16[20,16,8,2048]{3,2,0,1:T(8,128)(2,1)} copy(bf16[20,16,8,2048]{3,2,1,0:T(8,128)(2,1)} %bitcast.68) | data formatting | bytes 20971520 | tf_op jit(solution)/shard_map/all_to_all | solution.py:27
  16.6 8.4 %all-to-all-start = ((bf16[160,16,2048]{2,0,1:T(8,128)(2,1)}), bf16[160,16,2048]{2,0,1:T(8,128)(2,1)}, u32[]{:S(2)}, u32[]{:S(2)}) async-start(bf16[160,16,2048]{2,0,1:T(8,128)(2,1)} %bitcast.67), calls=%async_computation | async-start | bytes 20971520 | tf_op jit(solution)/shard_map/all_to_all | solution.py:27
  26.4 12.5 %all-gather.2.cloned.1.call-done = bf16[2048,512]{1,0:T(8,128)(2,1)} async-done(((bf16[2048,256]{1,0:T(8,128)(2,1)}), bf16[2048,512]{1,0:T(8,128)(2,1)}) %all-gather.2.cloned.1.call-update) | async-done | bytes 2097168 | tf_op jit(solution)/shard_map/all_gather | solution.py:18
  38.9 5.2 fusion.28
  44.1 178.5 %all-to-all-done = bf16[160,16,2048]{2,0,1:T(8,128)(2,1)} async-done(((bf16[160,16,2048]{2,0,1:T(8,128)(2,1)}), bf16[160,16,2048]{2,0,1:T(8,128)(2,1)}, u32[]{:S(2)}, u32[]{:S(2)}) %all-to-all-start) | async-done | bytes 10485792 | tf_op jit(solution)/shard_map/all_to_all | solution.py:27
  222.6 10.8 %fusion.27 = f32[512,2560]{1,0:T(8,128)} fusion(bf16[2560,2048]{1,0:T(8,128)(2,1)} %bitcast.10, bf16[2048,512]{1,0:T(8,128)(2,1)S(1)} %copy-done.1, pred[2048]{0:T(1024)(128)(4,1)S(1)} %iota_compare_fusion.3), kind=kOutput, calls=%fused_computation.43 | convolution fusion | flops 5369757696 | bytes 17827840 | tf_op jit(solution)/shard_map/dot_general | solution.py:31
  233.5 251.7 %all-reduce.4.cloned.1.call-done = (f32[512,2560]{1,0:T(8,128)}, f32[512,512]{0,1:T(8,128)}) async-done(((f32[512,2560]{1,0:T(8,128)}, f32[512,512]{0,1:T(8,128)}), (f32[512,2560]{1,0:T(8,128)}, f32[512,512]{0,1:T(8,128)})) %all-reduce.4.cloned.1.call-update) | async-done | bytes 6291472 | tf_op jit(solution)/shard_map/psum | solution.py:32
  487.1 11.7 %cholesky.104 = f32[128,128]{1,0:T(8,128)S(1)} custom-call(f32[128,128]{1,0:T(8,128)S(1)} %cholesky.266), custom_call_target="Cholesky" | custom-call | tf_op jit(solution)/shard_map/jit(cholesky)/cholesky | solution.py:29
  498.9 9.8 %custom-call.32 = f32[1,128,128]{1,2,0:T(8,128)S(1)} custom-call(f32[1,128,128]{2,1,0:T(8,128)S(1)} %get-tuple-element.34), custom_call_target="InvertDiagBlocksLowerTriangular" | custom-call | tf_op jit(solution)/shard_map/jit(cholesky)/cholesky | solution.py:29
  509.4 11.7 %cholesky.217 = f32[128,128]{1,0:T(8,128)S(1)} custom-call(f32[128,128]{1,0:T(8,128)S(1)} %cholesky.270), custom_call_target="Cholesky" | custom-call | tf_op jit(solution)/shard_map/jit(cholesky)/cholesky | solution.py:29
  521.2 10.2 %custom-call.33 = f32[1,128,128]{1,2,0:T(8,128)S(1)} custom-call(f32[1,128,128]{2,1,0:T(8,128)S(1)} %get-tuple-element.31), custom_call_target="InvertDiagBlocksLowerTriangular" | custom-call | tf_op jit(solution)/shard_map/jit(cholesky)/cholesky | solution.py:29
  532.0 11.7 %cholesky.238 = f32[128,128]{1,0:T(8,128)S(1)} custom-call(f32[128,128]{1,0:T(8,128)S(1)} %cholesky.275), custom_call_target="Cholesky" | custom-call | tf_op jit(solution)/shard_map/jit(cholesky)/cholesky | solution.py:29
  543.8 9.8 %custom-call.34 = f32[1,128,128]{1,2,0:T(8,128)S(1)} custom-call(f32[1,128,128]{2,1,0:T(8,128)S(1)} %get-tuple-element.28), custom_call_target="InvertDiagBlocksLowerTriangular" | custom-call | tf_op jit(solution)/shard_map/jit(cholesky)/cholesky | solution.py:29
  554.2 11.7 %cholesky.255 = f32[128,128]{1,0:T(8,128)S(1)} custom-call(f32[128,128]{1,0:T(8,128)S(1)} %convolution_subtract_fusion.6), custom_call_target="Cholesky" | custom-call | tf_op jit(solution)/shard_map/jit(cholesky)/cholesky | solution.py:29
  570.9 10.6 %while.1 = (s32[]{:T(128)}, f32[512,512]{1,0:T(8,128)S(1)}, s32[4,2]{0,1:T(2,128)S(1)}, f32[4,128,128]{2,1,0:T(8,128)}, s32[]{:T(128)}) while((s32[]{:T(128)}, f32[512,512]{1,0:T(8,128)S(1)}, s32[4,2]{0,1:T(2,128)S(1)}, f32[4,128,128]{2,1,0:T(8,128)}, s32[]{:T(128)}) %tuple.27), condition=%wide.while_cond, body=%wide.while_body.sunk | while | flops 2 | bytes 132205 | solution.py:11
  571.6 2.0 bitcast_dynamic-update-slice_fusion.2
  574.2 2.0 bitcast_dynamic-update-slice_fusion.2
  576.8 2.0 bitcast_dynamic-update-slice_fusion.2
  579.5 2.0 bitcast_dynamic-update-slice_fusion.2
  581.5 40.1 %custom-call.35 = f32[4,128,128]{1,2,0:T(8,128)S(1)} custom-call(f32[4,128,128]{2,1,0:T(8,128)} %get-tuple-element.12), custom_call_target="InvertDiagBlocksLowerTriangular" | custom-call | tf_op jit(solution)/shard_map/triangular_solve | solution.py:11
  621.6 2.7 fusion.24
  624.3 2.6 convolution_subtract_fusion.1
  631.0 2.5 fusion.15
  641.7 2.5 fusion.12
  (56 shorter events, 24.1 us)
Async XLA Ops:
  16.6 206.0 %all-to-all-start = ((bf16[160,16,2048]{2,0,1:T(8,128)(2,1)}), bf16[160,16,2048]{2,0,1:T(8,128)(2,1)}, u32[]{:S(2)}, u32[]{:S(2)}) async-start(bf16[160,16,2048]{2,0,1:T(8,128)(2,1)} %bitcast.67), calls=%async_computation | async-start | bytes 20971520 | tf_op jit(solution)/shard_map/all_to_all | solution.py:27
  24.9 14.0 %all-gather.2.cloned.1.call-start = ((), (), s32[]{:S(2)}) async-start(), calls=%async_computation.1 | async-start | bytes 3145728 | tf_op jit(solution)/shard_map/all_gather | solution.py:18
  25.7 459.5 %all-reduce.4.cloned.1.call-start = ((), (), s32[]{:S(2)}) async-start(), calls=%async_computation.2 | async-start | bytes 12582912 | tf_op jit(solution)/shard_map/psum | solution.py:32
  38.9 183.7 %copy-start.1 = (bf16[2048,512]{1,0:T(8,128)(2,1)S(1)}, bf16[2048,512]{1,0:T(8,128)(2,1)}, u32[]{:S(2)}) copy-start(bf16[2048,512]{1,0:T(8,128)(2,1)} %all-gather.2.cloned.1.call-done) | copy-start | bytes 6291460
  485.2 1.7 copy-start
  531.6 96.5 %slice-start = ((s8[5242880]{0:T(1024)(128)(4,1)}), s8[1048576]{0:T(1024)(128)(4,1)S(1)}, s32[]{:S(2)}) async-start(s8[5242880]{0:T(1024)(128)(4,1)} %bitcast.69), calls=%async_computation.3 | async-start | bytes 2097152
  621.6 6.6 %slice-start.1 = ((s8[5242880]{0:T(1024)(128)(4,1)}), s8[4194304]{0:T(1024)(128)(4,1)S(1)}, s32[]{:S(2)}) async-start(s8[5242880]{0:T(1024)(128)(4,1)} %bitcast.69), calls=%async_computation.4 | async-start | bytes 8388608
Sparse Core Ops, SparseCore 0:
  27.3 11.5 all-gather.1
  233.6 251.5 all-reduce.3
where the time goes:
time: 659 us; the launch traced here: 653 us
  waiting for transfers between devices  443 us (67%)
  other arithmetic  120 us (18%)
  matrix products  41.6 us (6%)
  local copies, waits for them, and re-layouts  22.4 us (3%)
  between operations  17.2 us (3%)
  starting transfers between devices  8.44 us (1%)
    psum x1, waiting for transfers between devices, shards(): cross_sum = lax.psum(cross_local, 'donor')  252 us
    all_to_all x1, waiting for transfers between devices, shards(): lax.all_to_all(targets_by_gene, 'donor', split_axis=1, concat_axis=0, til...  178 us
    another operation x14, other arithmetic, shards(): lower_factor = jnp.linalg.cholesky(gram_matrix)  78.9 us
    another operation x3, other arithmetic, solve_both(): lax.linalg.triangular_solve(lower_factor, halfway, left_side=True, lower=...  40.4 us
  transfers between devices with their start and end apart: 3, of which 3 were waited for; matrix products, arithmetic and copies ran while one was open for 1% of the time, Pallas kernels for 0%

commit v1 on v0

--- a/solution.py
+++ b/solution.py
@@ -1,9 +1,16 @@
+import functools
 import math
 
 import jax
 import jax.numpy as jnp
 from jax import lax
+from jax.experimental import pallas as pl
+from jax.experimental.pallas import tpu as pltpu
 from jax.sharding import PartitionSpec as P
+
+AXES = ("donor", "gene")
+HI = lax.Precision.HIGHEST
+VMEM_BYTES = 48 * 1024 * 1024
 
 
 def solve_both(lower_factor, right_cols):
@@ -13,7 +20,7 @@
     )
 
 
-def shards(embeddings, targets_by_gene, cell_counts):
+def shards_any_mesh(embeddings, targets_by_gene, cell_counts):
     valid_count = cell_counts[0]
     gathered = lax.all_gather(embeddings, "gene", axis=1, tiled=True)
     row_total = gathered.shape[0]
@@ -36,8 +43,220 @@
     return lax.dynamic_slice_in_dim(scaled, first_row, share, 0)
 
 
+def permutation(target):
+    pairs = []
+    for z in range(4):
+        for y in range(2):
+            for x in range(2):
+                for c in range(2):
+                    there = target(z, y, x, c)
+                    if there is not None:
+                        tz, ty, tx, tc = there
+                        pairs.append((((z * 2 + y) * 2 + x) * 2 + c, ((tz * 2 + ty) * 2 + tx) * 2 + tc))
+    return pairs
+
+
+CORE = permutation(lambda z, y, x, c: (z, y, x, 1 - c))
+NEAR = permutation(lambda z, y, x, c: (z, y, 1 - x, c) if c == 0 else (z, 1 - y, x, c))
+FAR = permutation(lambda z, y, x, c: (z, 1 - y, x, c) if c == 0 else (z, y, 1 - x, c))
+DIAG_OUT = permutation(lambda z, y, x, c: (z, 1 - y, x, 1) if c == 0 else (z, y, 1 - x, 0))
+DIAG_BACK = permutation(lambda z, y, x, c: (z, y, 1 - x, 1) if c == 0 else (z, 1 - y, x, 0))
+UP = permutation(lambda z, y, x, c: (z + 1, y, x, c) if z < 3 else None)
+DOWN = permutation(lambda z, y, x, c: (z - 1, y, x, c) if z > 0 else None)
+ZXOR = [permutation(lambda z, y, x, c, s=s: (z ^ s, y, x, c)) for s in (1, 2, 3)]
+
+
+def send(value, perm):
+    return lax.ppermute(value, AXES, perm)
+
+
+def pick_kernel(index_ref, t_ref, o_ref):
+    o_ref[0] = t_ref[...]
+
+
+def pick_blocks(targets, block_index, block_cells):
+    rows = targets.shape[0]
+    count = block_index.shape[0]
+    return pl.pallas_call(
+        pick_kernel,
+        out_shape=jax.ShapeDtypeStruct((count, rows, block_cells), targets.dtype),
+        grid_spec=pltpu.PrefetchScalarGridSpec(
+            num_scalar_prefetch=1,
+            grid=(count,),
+            in_specs=[pl.BlockSpec((rows, block_cells), lambda k, index: (0, index[k]))],
+            out_specs=pl.BlockSpec((1, rows, block_cells), lambda k, index: (k, 0, 0)),
+        ),
+        cost_estimate=pl.CostEstimate(
+            flops=0, bytes_accessed=4 * count * rows * block_cells, transcendentals=0
+        ),
+        name="pick_blocks",
+    )(block_index, targets)
+
+
+def cross_kernel(index_ref, own_ref, core_ref, near_ref, diag_ref, x_ref, *rest):
+    prior_ref, o_ref = rest if len(rest) == 2 else (None, rest[0])
+    rows = own_ref.shape[0]
+    block = x_ref[...]
+    for q, piece in enumerate((own_ref[...], core_ref[0], near_ref[0], diag_ref[0])):
+        part = jnp.dot(piece, block, preferred_element_type=jnp.float32)
+        place = pl.ds(q * rows, rows)
+        if prior_ref is not None:
+            part = part + prior_ref[place, :]
+        o_ref[place, :] = part
+
+
+def cross_add(prior, block_index, slot, targets, from_core, from_near, from_diag, block):
+    rows = targets.shape[0]
+    cells, width = block.shape
+    index = jnp.stack([block_index, slot]).astype(jnp.int32)
+    piece = pl.BlockSpec((1, rows, cells), lambda i, index: (index[1], 0, 0))
+    whole = lambda shape: pl.BlockSpec(shape, lambda i, index: (0, 0))
+    in_specs = [
+        pl.BlockSpec((rows, cells), lambda i, index: (0, index[0])),
+        piece,
+        piece,
+        piece,
+        whole((cells, width)),
+    ]
+    operands = [index, targets, from_core, from_near, from_diag, block]
+    aliases = {}
+    if prior is not None:
+        in_specs.append(whole((4 * rows, width)))
+        operands.append(prior)
+        aliases = {6: 0}
+    return pl.pallas_call(
+        cross_kernel,
+        out_shape=jax.ShapeDtypeStruct((4 * rows, width), jnp.float32),
+        grid_spec=pltpu.PrefetchScalarGridSpec(
+            num_scalar_prefetch=1,
+            grid=(1,),
+            in_specs=in_specs,
+            out_specs=whole((4 * rows, width)),
+        ),
+        input_output_aliases=aliases,
+        compiler_params=pltpu.CompilerParams(vmem_limit_bytes=VMEM_BYTES),
+        cost_estimate=pl.CostEstimate(
+            flops=8 * rows * cells * width, bytes_accessed=8 * rows * cells + 2 * cells * width, transcendentals=0
+        ),
+        name="cross_add",
+    )(*operands)
+
+
+def halves(value, bit):
+    half = value.shape[0] // 2
+    keep = lax.dynamic_slice_in_dim(value, bit * half, half, 0)
+    give = lax.dynamic_slice_in_dim(value, (1 - bit) * half, half, 0)
+    return keep, give
+
+
+def join(mine, other, bit):
+    low = jnp.where(bit == 0, mine, other)
+    high = jnp.where(bit == 0, other, mine)
+    return jnp.concatenate([low, high], axis=0)
+
+
+def sum_everywhere(value, z, c, near_bit, far_bit):
+    for bit, perm in ((c, CORE), (near_bit, NEAR), (far_bit, FAR)):
+        keep, give = halves(value, bit)
+        value = keep + send(give, perm)
+    quarter = value.shape[0] // 4
+    part = lambda i: lax.dynamic_slice_in_dim(value, i * quarter, quarter, 0)
+    total = part(z)
+    for s in (1, 2, 3):
+        total = total + send(part(z ^ s), ZXOR[s - 1])
+    parts = jnp.zeros_like(value)
+    parts = lax.dynamic_update_slice_in_dim(parts, total, z * quarter, 0)
+    for s in (1, 2, 3):
+        parts = lax.dynamic_update_slice_in_dim(parts, send(total, ZXOR[s - 1]), (z ^ s) * quarter, 0)
+    value = parts
+    for bit, perm in ((far_bit, FAR), (near_bit, NEAR), (c, CORE)):
+        value = join(value, send(value, perm), bit)
+    return value
+
+
+def shards(embeddings, targets_by_gene, cell_counts):
+    slots = embeddings.shape[0]
+    donors = lax.axis_size("donor")
+    donor = lax.axis_index("donor")
+    c = lax.axis_index("gene")
+    z, y, x = donor // 4, (donor // 2) % 2, donor % 2
+    near_bit = jnp.where(c == 0, x, y)
+    far_bit = jnp.where(c == 0, y, x)
+    half = slots // 2
+
+    row_valid = lax.broadcasted_iota(jnp.int32, (slots, 1), 0) < cell_counts[0]
+    masked = jnp.where(row_valid, embeddings, jnp.zeros_like(embeddings))
+    keep, give = halves(masked, c)
+    got = send(give, CORE)
+    block = jnp.concatenate(
+        [jnp.where(c == 0, keep, got), jnp.where(c == 0, got, keep)], axis=1
+    )
+
+    def group_donor(k, core, bit):
+        line, other = k // 2, k % 2
+        return line * 4 + jnp.where(core == 0, other * 2 + bit, bit * 2 + other)
+
+    ks = jnp.arange(8, dtype=jnp.int32)
+
+    def blocks_for(core, bit):
+        return (group_donor(ks, core, bit) * 2 + core).astype(jnp.int32)
+
+    far_bit_there = jnp.where(c == 0, y, x)
+    from_near = send(pick_blocks(targets_by_gene, blocks_for(c, 1 - near_bit), half), NEAR)
+    from_diag = send(pick_blocks(targets_by_gene, blocks_for(1 - c, 1 - far_bit_there), half), DIAG_OUT)
+    from_core = send(pick_blocks(targets_by_gene, blocks_for(1 - c, far_bit_there), half), CORE)
+
+    up1 = send(block, UP)
+    down1 = send(block, DOWN)
+    up2 = send(up1, UP)
+    down2 = send(down1, DOWN)
+    up3 = send(up2, UP)
+    down3 = send(down2, DOWN)
+    near_z = jnp.where(z == 0, down1, up1)
+    mid_z = jnp.where(z <= 1, down2, up2)
+    last_z = jnp.where(z == 0, down3, jnp.where(z == 3, up3, down1))
+    lines = (
+        (block, z),
+        (near_z, jnp.where(z == 0, 1, z - 1)),
+        (mid_z, jnp.where(z <= 1, z + 2, z - 2)),
+        (last_z, jnp.where(z == 0, 3, jnp.where(z == 3, 0, z + 1))),
+    )
+    pieces = [(value, line, far_bit) for value, line in lines]
+    pieces += [(send(value, FAR), line, 1 - far_bit) for value, line in lines]
+
+    gram_matrix = lax.dot_general(
+        block, block, (((0,), (0,)), ((), ())), preferred_element_type=jnp.float32
+    )
+    gram_matrix = sum_everywhere(gram_matrix, z, c, near_bit, far_bit)
+    lower_factor = jnp.linalg.cholesky(gram_matrix)
+    width = gram_matrix.shape[0]
+    lower_inverse = lax.linalg.triangular_solve(
+        lower_factor, jnp.eye(width, dtype=jnp.float32), left_side=True, lower=True
+    )
+
+    acc = None
+    for value, line, other in pieces:
+        k = line * 2 + other
+        acc = cross_add(
+            acc, group_donor(k, c, near_bit) * 2 + c, k, targets_by_gene, from_core, from_near, from_diag, value
+        )
+    rows = targets_by_gene.shape[0]
+    part = lambda q: acc[q * rows : (q + 1) * rows]
+    cross = part(0) + send(part(1), CORE) + send(part(2), NEAR) + send(part(3), DIAG_BACK)
+
+    dims = lambda a, b: (((a,), (b,)), ((), ()))
+    halfway = lax.dot_general(lower_inverse, cross, dims(1, 1), precision=HI)
+    scaled = math.sqrt(slots * donors) * lax.dot_general(lower_inverse, halfway, dims(0, 0), precision=HI)
+    return lax.all_to_all(scaled, "donor", split_axis=0, concat_axis=1, tiled=True)
+
+
 def solution(mesh):
     placed = (P("donor", "gene"), P(("gene", "donor"), None), P("donor"))
+    tuned = mesh.shape["donor"] == 16 and mesh.shape["gene"] == 2
     return jax.shard_map(
-        shards, mesh=mesh, in_specs=placed, out_specs=P("donor", "gene"), check_vma=False
-    )
+        shards if tuned else shards_any_mesh,
+        mesh=mesh,
+        in_specs=placed,
+        out_specs=P("donor", "gene"),
+        check_vma=False,
+    )

time: 659 us -> 393 us (0.60)
  waiting for transfers between devices: 443 us -> 82.8 us
  Pallas kernels: 0 us -> 41.4 us
  starting transfers between devices: 8.44 us -> 46.6 us
  matrix products: 41.6 us -> 17.3 us
  other arithmetic: 120 us -> 144 us
  blocking collectives: 0 us -> 20 us
  between operations: 17.2 us -> 4.16 us
  local copies, waits for them, and re-layouts: 22.4 us -> 30 us
    psum x1 -> x0, waiting for transfers between devices: 252 us -> none  [shards(): cross_sum = lax.psum(cross_local, 'donor')]
    all_to_all x1 -> x0, waiting for transfers between devices: 178 us -> none  [shards(): lax.all_to_all(targets_by_gene, 'donor', split_axis=1, concat_axis=0, til...]
    ppermute x0 -> x29, waiting for transfers between devices: none -> 82.8 us  [send(): return lax.ppermute(value, AXES, perm)]
    ppermute x0 -> x29, starting transfers between devices: none -> 46.6 us  [send(): return lax.ppermute(value, AXES, perm)]
    pallas_call x0 -> x11, Pallas kernels: none -> 41.4 us  [the longest x8 21.6 us: cross_add(): pl.pallas_call(cross_kernel, out_shape=jax.ShapeDtypeStruct((4 * rows, wi...]
    all_to_all x0 -> x1, blocking collectives: none -> 20 us  [shards(): lax.all_to_all(scaled, 'donor', split_axis=0, concat_axis=1, tiled=True)]
    another operation x14 -> x7, matrix products: 23.7 us -> 6.59 us  [shards(): lax.linalg.triangular_solve(lower_factor, jnp.eye(width, dtype=jnp.float3...]
    dot_general x2 -> x3, matrix products: 16.1 us -> 2.86 us  [the longest x1 1.29 us: shards(): halfway = lax.dot_general(lower_inverse, cross, dims(1, 1), precision=HI)]
  transfers between devices with their start and end apart: 3 -> 29, of which waited for: 3 -> 15; matrix products, arithmetic and copies ran while one was open for 1% -> 47% of each run, Pallas kernels for 0% -> 10%
where the time goes in v1:
time: 393 us; the launch traced here: 386 us
  other arithmetic  144 us (37%)
  waiting for transfers between devices  82.8 us (21%)
  starting transfers between devices  46.6 us (12%)
  Pallas kernels  41.4 us (11%)
  local copies, waits for them, and re-layouts  30 us (8%)
  blocking collectives  20 us (5%)
  matrix products  17.3 us (4%)
  between operations  4.16 us (1%)
    ppermute x29, waiting for transfers between devices, send(): return lax.ppermute(value, AXES, perm)  82.8 us
    another operation x14, other arithmetic, shards(): lower_factor = jnp.linalg.cholesky(gram_matrix)  80.9 us
    ppermute x29, starting transfers between devices, send(): return lax.ppermute(value, AXES, perm)  46.6 us
    another operation x3, other arithmetic, shards(): lax.linalg.triangular_solve(lower_factor, jnp.eye(width, dtype=jnp.float3...  42.5 us
    pallas_call x8, Pallas kernels, cross_add(): pl.pallas_call(cross_kernel, out_shape=jax.ShapeDtypeStruct((4 * rows, wi...  21.6 us
    all_to_all x1, blocking collectives, shards(): lax.all_to_all(scaled, 'donor', split_axis=0, concat_axis=1, tiled=True)  20 us
    pallas_call x3, Pallas kernels, pick_blocks(): pl.pallas_call(pick_kernel, out_shape=jax.ShapeDtypeStruct((count, rows,...  19.8 us
    another operation x12, local copies, waits for them, and re-layouts  14.1 us
  transfers between devices with their start and end apart: 29, of which 15 were waited for; matrix products, arithmetic and copies ran while one was open for 47% of the time, Pallas kernels for 10%

profile of v1, /device:TPU:0, one launch (start us, length us, event | category | flops | bytes accessed | tf_op | source)
XLA Modules:
  0.0 386.0 jit_solution(12612625835617780714)
XLA Ops:
  18.7 6.6 %pick_blocks.3 = bf16[8,160,1024]{2,1,0:T(8,128)(2,1)} custom-call(s32[8]{0:T(128)} %fusion.42.index_ref, bf16[160,32768]{1,0:T(8,128)(2,1)} %own_ref.15), custom_call_target="tpu_custom_call" | custom-call | bytes 5242880 | tf_op jit(solution)/shard_map/pick_blocks/pallas_call | solution.py:80
  25.8 6.6 %pick_blocks.4 = bf16[8,160,1024]{2,1,0:T(8,128)(2,1)} custom-call(s32[8]{0:T(128)} %fusion.40.index_ref, bf16[160,32768]{1,0:T(8,128)(2,1)} %own_ref.15), custom_call_target="tpu_custom_call" | custom-call | bytes 5242880 | tf_op jit(solution)/shard_map/pick_blocks/pallas_call | solution.py:80
  39.5 7.0 %collective-permute-done.6 = f32[16,512]{0,1:T(8,128)S(1)} collective-permute-done((f32[16,512]{0,1:T(8,128)}, f32[16,512]{0,1:T(8,128)S(1)}, u32[]{:S(2)}, u32[]{:S(2)}) %collective-permute-start.6) | collective-permute-done | bytes 32800 | tf_op jit(solution)/shard_map/ppermute | solution.py:70
  46.4 14.3 %collective-permute-done.5 = f32[16,512]{0,1:T(8,128)} collective-permute-done((f32[16,512]{0,1:T(8,128)}, f32[16,512]{0,1:T(8,128)}, u32[]{:S(2)}, u32[]{:S(2)}) %collective-permute-start.5) | collective-permute-done | bytes 32800 | tf_op jit(solution)/shard_map/ppermute | solution.py:70
  68.0 6.5 %collective-permute-done.7 = f32[16,512]{0,1:T(8,128)} collective-permute-done((f32[16,512]{0,1:T(8,128)S(1)}, f32[16,512]{0,1:T(8,128)}, u32[]{:S(2)}, u32[]{:S(2)}) %collective-permute-start.7) | collective-permute-done | bytes 32800 | tf_op jit(solution)/shard_map/ppermute | solution.py:70
  76.7 6.8 %collective-permute-done.8 = f32[16,512]{0,1:T(8,128)} collective-permute-done((f32[16,512]{0,1:T(8,128)S(1)}, f32[16,512]{0,1:T(8,128)}, u32[]{:S(2)}, u32[]{:S(2)}) %collective-permute-start.8) | collective-permute-done | bytes 32800 | tf_op jit(solution)/shard_map/ppermute | solution.py:70
  89.0 7.0 %collective-permute-done.10 = f32[64,512]{0,1:T(8,128)} collective-permute-done((f32[64,512]{0,1:T(8,128)S(1)}, f32[64,512]{0,1:T(8,128)}, u32[]{:S(2)}, u32[]{:S(2)}) %collective-permute-start.10) | collective-permute-done | bytes 131104 | tf_op jit(solution)/shard_map/ppermute | solution.py:70
  102.2 5.6 %collective-permute-start.19 = (bf16[1024,512]{1,0:T(8,128)(2,1)}, bf16[1024,512]{1,0:T(8,128)(2,1)}, u32[]{:S(2)}, u32[]{:S(2)}) collective-permute-start(bf16[1024,512]{1,0:T(8,128)(2,1)} %pad_maximum_fusion.x_ref), channel_id=1, source_target_pairs={{0,8},{1,9},{2,10},{3,11},{4,12},{5,13},{6,14},{7,15},{8,16},{9,17... | collective-permute-start | bytes 3145736 | tf_op jit(solution)/shard_map/ppermute | solution.py:70
  109.9 6.6 %pick_blocks.5 = bf16[8,160,1024]{2,1,0:T(8,128)(2,1)} custom-call(s32[8]{0:T(128)} %fusion.41.index_ref, bf16[160,32768]{1,0:T(8,128)(2,1)} %own_ref.15), custom_call_target="tpu_custom_call" | custom-call | bytes 5242880 | tf_op jit(solution)/shard_map/pick_blocks/pallas_call | solution.py:80
  118.6 6.2 %collective-permute-done.16 = bf16[1024,512]{1,0:T(8,128)(2,1)} collective-permute-done((bf16[1024,512]{1,0:T(8,128)(2,1)}, bf16[1024,512]{1,0:T(8,128)(2,1)}, u32[]{:S(2)}, u32[]{:S(2)}) %collective-permute-start.16) | collective-permute-done | bytes 1048608 | tf_op jit(solution)/shard_map/ppermute | solution.py:70
  127.3 6.2 %collective-permute-start.20 = (bf16[1024,512]{1,0:T(8,128)(2,1)}, bf16[1024,512]{1,0:T(8,128)(2,1)}, u32[]{:S(2)}, u32[]{:S(2)}) collective-permute-start(bf16[1024,512]{1,0:T(8,128)(2,1)} %collective-permute-done.19), channel_id=1, source_target_pairs={{0,8},{1,9},{2,10},{3,11},{4,12},{5,13},{6,14},{7,15},{8,16},{9,17... | collective-permute-start | bytes 3145736 | tf_op jit(solution)/shard_map/ppermute | solution.py:70
  141.6 11.7 %cholesky.104 = f32[128,128]{1,0:T(8,128)S(1)} custom-call(f32[128,128]{1,0:T(8,128)S(1)} %cholesky.266), custom_call_target="Cholesky" | custom-call | tf_op jit(solution)/shard_map/jit(cholesky)/cholesky | solution.py:231
  154.5 9.8 %custom-call.30 = f32[1,128,128]{1,2,0:T(8,128)S(1)} custom-call(f32[1,128,128]{2,1,0:T(8,128)S(1)} %get-tuple-element.48), custom_call_target="InvertDiagBlocksLowerTriangular" | custom-call | tf_op jit(solution)/shard_map/jit(cholesky)/cholesky | solution.py:231
  167.6 11.7 %cholesky.217 = f32[128,128]{1,0:T(8,128)S(1)} custom-call(f32[128,128]{1,0:T(8,128)S(1)} %cholesky.270), custom_call_target="Cholesky" | custom-call | tf_op jit(solution)/shard_map/jit(cholesky)/cholesky | solution.py:231
  179.9 10.0 %custom-call.31 = f32[1,128,128]{1,2,0:T(8,128)S(1)} custom-call(f32[1,128,128]{2,1,0:T(8,128)S(1)} %get-tuple-element.45), custom_call_target="InvertDiagBlocksLowerTriangular" | custom-call | tf_op jit(solution)/shard_map/jit(cholesky)/cholesky | solution.py:231
  192.3 11.7 %cholesky.238 = f32[128,128]{1,0:T(8,128)S(1)} custom-call(f32[128,128]{1,0:T(8,128)S(1)} %cholesky.275), custom_call_target="Cholesky" | custom-call | tf_op jit(solution)/shard_map/jit(cholesky)/cholesky | solution.py:231
  204.6 9.8 %custom-call.32 = f32[1,128,128]{1,2,0:T(8,128)S(1)} custom-call(f32[1,128,128]{2,1,0:T(8,128)S(1)} %get-tuple-element.42), custom_call_target="InvertDiagBlocksLowerTriangular" | custom-call | tf_op jit(solution)/shard_map/jit(cholesky)/cholesky | solution.py:231
  216.7 11.7 %cholesky.255 = f32[128,128]{1,0:T(8,128)S(1)} custom-call(f32[128,128]{1,0:T(8,128)S(1)} %convolution_subtract_fusion.5), custom_call_target="Cholesky" | custom-call | tf_op jit(solution)/shard_map/jit(cholesky)/cholesky | solution.py:231
  237.9 5.6 %collective-permute-start.21 = (bf16[1024,512]{1,0:T(8,128)(2,1)}, bf16[1024,512]{1,0:T(8,128)(2,1)}, u32[]{:S(2)}, u32[]{:S(2)}) collective-permute-start(bf16[1024,512]{1,0:T(8,128)(2,1)} %collective-permute-done.20), channel_id=1, source_target_pairs={{0,8},{1,9},{2,10},{3,11},{4,12},{5,13},{6,14},{7,15},{8,16},{9,17... | collective-permute-start | bytes 3145736 | tf_op jit(solution)/shard_map/ppermute | solution.py:70
  243.5 14.1 %while.1 = (s32[]{:T(128)}, f32[512,512]{1,0:T(8,128)}, s32[4,2]{0,1:T(2,128)S(1)}, f32[4,128,128]{2,1,0:T(8,128)}, s32[]{:T(128)}) while((s32[]{:T(128)}, f32[512,512]{1,0:T(8,128)}, s32[4,2]{0,1:T(2,128)S(1)}, f32[4,128,128]{2,1,0:T(8,128)}, s32[]{:T(128)}) %tuple.37), condition=%wide.while_cond, body=%wide.while_body.sunk | while | flops 2 | bytes 132205 | solution.py:233
  257.5 40.1 %custom-call.33 = f32[4,128,128]{1,2,0:T(8,128)S(1)} custom-call(f32[4,128,128]{2,1,0:T(8,128)} %get-tuple-element.12), custom_call_target="InvertDiagBlocksLowerTriangular" | custom-call | tf_op jit(solution)/shard_map/triangular_solve | solution.py:233
  329.1 8.6 %collective-permute-done.23.x_ref = bf16[1024,512]{1,0:T(8,128)(2,1)S(1)} collective-permute-done((bf16[1024,512]{1,0:T(8,128)(2,1)S(1)}, bf16[1024,512]{1,0:T(8,128)(2,1)S(1)}, u32[]{:S(2)}, u32[]{:S(2)}) %collective-permute-start.23) | collective-permute-done | bytes 1048608 | tf_op jit(solution)/shard_map/ppermute | solution.py:70
  340.4 8.6 %collective-permute-done.22.x_ref = bf16[1024,512]{1,0:T(8,128)(2,1)S(1)} collective-permute-done((bf16[1024,512]{1,0:T(8,128)(2,1)S(1)}, bf16[1024,512]{1,0:T(8,128)(2,1)S(1)}, u32[]{:S(2)}, u32[]{:S(2)}) %collective-permute-start.22) | collective-permute-done | bytes 1048608 | tf_op jit(solution)/shard_map/ppermute | solution.py:70
  364.5 20.0 %all_to_all.19 = f32[16,32,160]{2,1,0:T(8,128)S(1)} all-to-all(f32[16,32,160]{2,1,0:T(8,128)S(1)} %bitcast.69), channel_id=1, replica_groups=mesh['donor'=16,'gene'=2] {'donor'}, dimensions={0} | all-to-all | bytes 655360 | tf_op jit(solution)/shard_map/all_to_all | solution.py:250
  (160 shorter events, 143.3 us)
Async XLA Ops:
  16.1 17.8 %collective-permute-start.3 = (f32[64,512]{0,1:T(8,128)S(1)}, f32[64,512]{0,1:T(8,128)S(1)}, u32[]{:S(2)}, u32[]{:S(2)}) collective-permute-start(f32[64,512]{0,1:T(8,128)S(1)} %constant_dynamic-slice_fusion.4), channel_id=1, source_target_pairs={{0,4},{1,3},{2,6},{3,1},{4,0},{5,7},{6,2},{7,5},{8,12},{9,11},{10,... | collective-permute-start | bytes 393224 | tf_op jit(solution)/shard_map/ppermute | solution.py:70
  25.3 280.1 %collective-permute-start.13 = (bf16[8,160,1024]{2,1,0:T(8,128)(2,1)}, bf16[8,160,1024]{2,1,0:T(8,128)(2,1)S(1)}, u32[]{:S(2)}, u32[]{:S(2)}) collective-permute-start(bf16[8,160,1024]{2,1,0:T(8,128)(2,1)} %pick_blocks.3), channel_id=1, source_target_pairs={{0,1},{1,0},{2,3},{3,2},{4,5},{5,4},{6,7},{7,6},{8,9},{9,8},{10,11... | collective-permute-start | bytes 7864328 | tf_op jit(solution)/shard_map/ppermute | solution.py:70
  32.4 273.8 %collective-permute-start.14 = (bf16[8,160,1024]{2,1,0:T(8,128)(2,1)}, bf16[8,160,1024]{2,1,0:T(8,128)(2,1)}, u32[]{:S(2)}, u32[]{:S(2)}) collective-permute-start(bf16[8,160,1024]{2,1,0:T(8,128)(2,1)} %pick_blocks.4), channel_id=1, source_target_pairs={{0,2},{1,5},{2,0},{3,7},{4,6},{5,1},{6,4},{7,3},{8,10},{9,13},{10,... | collective-permute-start | bytes 7864328 | tf_op jit(solution)/shard_map/ppermute | solution.py:70
  35.1 11.3 %collective-permute-start.6 = (f32[16,512]{0,1:T(8,128)}, f32[16,512]{0,1:T(8,128)S(1)}, u32[]{:S(2)}, u32[]{:S(2)}) collective-permute-start(f32[16,512]{0,1:T(8,128)} %get-tuple-element.37), channel_id=1, source_target_pairs={{0,24},{1,25},{2,26},{3,27},{4,28},{5,29},{6,30},{7,31},{8,16},{9,... | collective-permute-start | bytes 98312 | tf_op jit(solution)/shard_map/ppermute | solution.py:70
  38.7 22.0 %collective-permute-start.5 = (f32[16,512]{0,1:T(8,128)}, f32[16,512]{0,1:T(8,128)}, u32[]{:S(2)}, u32[]{:S(2)}) collective-permute-start(f32[16,512]{0,1:T(8,128)} %get-tuple-element.38), channel_id=1, source_target_pairs={{0,16},{1,17},{2,18},{3,19},{4,20},{5,21},{6,22},{7,23},{8,24},{9,... | collective-permute-start | bytes 98312 | tf_op jit(solution)/shard_map/ppermute | solution.py:70
  38.7 22.0 %collective-permute-start.4 = (f32[16,512]{0,1:T(8,128)S(1)}, f32[16,512]{0,1:T(8,128)}, u32[]{:S(2)}, u32[]{:S(2)}) collective-permute-start(f32[16,512]{0,1:T(8,128)S(1)} %get-tuple-element.36), channel_id=1, source_target_pairs={{0,8},{1,9},{2,10},{3,11},{4,12},{5,13},{6,14},{7,15},{8,0},{9,1},... | collective-permute-start | bytes 98312 | tf_op jit(solution)/shard_map/ppermute | solution.py:70
  61.9 12.6 %collective-permute-start.7 = (f32[16,512]{0,1:T(8,128)S(1)}, f32[16,512]{0,1:T(8,128)}, u32[]{:S(2)}, u32[]{:S(2)}) collective-permute-start(f32[16,512]{0,1:T(8,128)S(1)} %add_add_fusion), channel_id=1, source_target_pairs={{0,8},{1,9},{2,10},{3,11},{4,12},{5,13},{6,14},{7,15},{8,0},{9,1},... | collective-permute-start | bytes 98312 | tf_op jit(solution)/shard_map/ppermute | solution.py:70
  62.0 21.6 %collective-permute-start.8 = (f32[16,512]{0,1:T(8,128)S(1)}, f32[16,512]{0,1:T(8,128)}, u32[]{:S(2)}, u32[]{:S(2)}) collective-permute-start(f32[16,512]{0,1:T(8,128)S(1)} %add_add_fusion), channel_id=1, source_target_pairs={{0,16},{1,17},{2,18},{3,19},{4,20},{5,21},{6,22},{7,23},{8,24},{9,... | collective-permute-start | bytes 98312 | tf_op jit(solution)/shard_map/ppermute | solution.py:70
  65.0 20.8 %collective-permute-start.9 = (f32[16,512]{0,1:T(8,128)S(1)}, f32[16,512]{0,1:T(8,128)S(1)}, u32[]{:S(2)}, u32[]{:S(2)}) collective-permute-start(f32[16,512]{0,1:T(8,128)S(1)} %add_add_fusion), channel_id=1, source_target_pairs={{0,24},{1,25},{2,26},{3,27},{4,28},{5,29},{6,30},{7,31},{8,16},{9,... | collective-permute-start | bytes 98312 | tf_op jit(solution)/shard_map/ppermute | solution.py:70
  87.3 8.8 %collective-permute-start.10 = (f32[64,512]{0,1:T(8,128)S(1)}, f32[64,512]{0,1:T(8,128)}, u32[]{:S(2)}, u32[]{:S(2)}) collective-permute-start(f32[64,512]{0,1:T(8,128)S(1)} %dynamic_update_slice.15), channel_id=1, source_target_pairs={{0,4},{1,3},{2,6},{3,1},{4,0},{5,7},{6,2},{7,5},{8,12},{9,11},{10,... | collective-permute-start | bytes 393224 | tf_op jit(solution)/shard_map/ppermute | solution.py:70
  97.2 10.6 %collective-permute-start.11 = (f32[128,512]{0,1:T(8,128)S(1)}, f32[128,512]{0,1:T(8,128)}, u32[]{:S(2)}, u32[]{:S(2)}) collective-permute-start(f32[128,512]{0,1:T(8,128)S(1)} %pad_maximum_fusion.6), channel_id=1, source_target_pairs={{0,2},{1,5},{2,0},{3,7},{4,6},{5,1},{6,4},{7,3},{8,10},{9,13},{10,... | collective-permute-start | bytes 786440 | tf_op jit(solution)/shard_map/ppermute | solution.py:70
  100.9 23.9 %collective-permute-start.16 = (bf16[1024,512]{1,0:T(8,128)(2,1)}, bf16[1024,512]{1,0:T(8,128)(2,1)}, u32[]{:S(2)}, u32[]{:S(2)}) collective-permute-start(bf16[1024,512]{1,0:T(8,128)(2,1)} %pad_maximum_fusion.x_ref), channel_id=1, source_target_pairs={{8,0},{9,1},{10,2},{11,3},{12,4},{13,5},{14,6},{15,7},{16,8},{17,9... | collective-permute-start | bytes 3145736 | tf_op jit(solution)/shard_map/ppermute | solution.py:70
  102.2 23.8 %collective-permute-start.19 = (bf16[1024,512]{1,0:T(8,128)(2,1)}, bf16[1024,512]{1,0:T(8,128)(2,1)}, u32[]{:S(2)}, u32[]{:S(2)}) collective-permute-start(bf16[1024,512]{1,0:T(8,128)(2,1)} %pad_maximum_fusion.x_ref), channel_id=1, source_target_pairs={{0,8},{1,9},{2,10},{3,11},{4,12},{5,13},{6,14},{7,15},{8,16},{9,17... | collective-permute-start | bytes 3145736 | tf_op jit(solution)/shard_map/ppermute | solution.py:70
  109.8 17.4 %collective-permute-start.12 = (f32[256,512]{0,1:T(8,128)}, f32[256,512]{0,1:T(8,128)}, u32[]{:S(2)}, u32[]{:S(2)}) collective-permute-start(f32[256,512]{0,1:T(8,128)} %pad_maximum_fusion.5), channel_id=1, source_target_pairs={{0,1},{1,0},{2,3},{3,2},{4,5},{5,4},{6,7},{7,6},{8,9},{9,8},{10,11... | collective-permute-start | bytes 1572872 | tf_op jit(solution)/shard_map/ppermute | solution.py:70
  124.8 184.9 %collective-permute-start.15 = (bf16[8,160,1024]{2,1,0:T(8,128)(2,1)}, bf16[8,160,1024]{2,1,0:T(8,128)(2,1)}, u32[]{:S(2)}, u32[]{:S(2)}) collective-permute-start(bf16[8,160,1024]{2,1,0:T(8,128)(2,1)} %pick_blocks.5), channel_id=1, source_target_pairs={{0,5},{1,2},{2,7},{3,0},{4,1},{5,6},{6,3},{7,4},{8,13},{9,10},{10,... | collective-permute-start | bytes 7864328 | tf_op jit(solution)/shard_map/ppermute | solution.py:70
  126.0 110.6 %collective-permute-start.17 = (bf16[1024,512]{1,0:T(8,128)(2,1)}, bf16[1024,512]{1,0:T(8,128)(2,1)}, u32[]{:S(2)}, u32[]{:S(2)}) collective-permute-start(bf16[1024,512]{1,0:T(8,128)(2,1)} %collective-permute-done.16), channel_id=1, source_target_pairs={{8,0},{9,1},{10,2},{11,3},{12,4},{13,5},{14,6},{15,7},{16,8},{17,9... | collective-permute-start | bytes 3145736 | tf_op jit(solution)/shard_map/ppermute | solution.py:70
  127.3 110.6 %collective-permute-start.20 = (bf16[1024,512]{1,0:T(8,128)(2,1)}, bf16[1024,512]{1,0:T(8,128)(2,1)}, u32[]{:S(2)}, u32[]{:S(2)}) collective-permute-start(bf16[1024,512]{1,0:T(8,128)(2,1)} %collective-permute-done.19), channel_id=1, source_target_pairs={{0,8},{1,9},{2,10},{3,11},{4,12},{5,13},{6,14},{7,15},{8,16},{9,17... | collective-permute-start | bytes 3145736 | tf_op jit(solution)/shard_map/ppermute | solution.py:70
  236.6 63.5 %collective-permute-start.18 = (bf16[1024,512]{1,0:T(8,128)(2,1)}, bf16[1024,512]{1,0:T(8,128)(2,1)}, u32[]{:S(2)}, u32[]{:S(2)}) collective-permute-start(bf16[1024,512]{1,0:T(8,128)(2,1)} %collective-permute-done.17), channel_id=1, source_target_pairs={{8,0},{9,1},{10,2},{11,3},{12,4},{13,5},{14,6},{15,7},{16,8},{17,9... | collective-permute-start | bytes 3145736 | tf_op jit(solution)/shard_map/ppermute | solution.py:70
  237.9 63.1 %collective-permute-start.21 = (bf16[1024,512]{1,0:T(8,128)(2,1)}, bf16[1024,512]{1,0:T(8,128)(2,1)}, u32[]{:S(2)}, u32[]{:S(2)}) collective-permute-start(bf16[1024,512]{1,0:T(8,128)(2,1)} %collective-permute-done.20), channel_id=1, source_target_pairs={{0,8},{1,9},{2,10},{3,11},{4,12},{5,13},{6,14},{7,15},{8,16},{9,17... | collective-permute-start | bytes 3145736 | tf_op jit(solution)/shard_map/ppermute | solution.py:70
  300.1 20.6 %collective-permute-start.25 = (bf16[1024,512]{1,0:T(8,128)(2,1)}, bf16[1024,512]{1,0:T(8,128)(2,1)S(1)}, u32[]{:S(2)}, u32[]{:S(2)}) collective-permute-start(bf16[1024,512]{1,0:T(8,128)(2,1)} %pad_maximum_fusion.x_ref), channel_id=1, source_target_pairs={{0,4},{1,3},{2,6},{3,1},{4,0},{5,7},{6,2},{7,5},{8,12},{9,11},{10,... | collective-permute-start | bytes 3145736 | tf_op jit(solution)/shard_map/ppermute | solution.py:70
  302.7 23.7 %collective-permute-start.24 = (bf16[1024,512]{1,0:T(8,128)(2,1)S(1)}, bf16[1024,512]{1,0:T(8,128)(2,1)S(1)}, u32[]{:S(2)}, u32[]{:S(2)}) collective-permute-start(bf16[1024,512]{1,0:T(8,128)(2,1)S(1)} %get-tuple-element.28.x_ref), channel_id=1, source_target_pairs={{0,4},{1,3},{2,6},{3,1},{4,0},{5,7},{6,2},{7,5},{8,12},{9,11},{10,... | collective-permute-start | bytes 3145736 | tf_op jit(solution)/shard_map/ppermute | solution.py:70
  305.4 32.3 %collective-permute-start.23 = (bf16[1024,512]{1,0:T(8,128)(2,1)S(1)}, bf16[1024,512]{1,0:T(8,128)(2,1)S(1)}, u32[]{:S(2)}, u32[]{:S(2)}) collective-permute-start(bf16[1024,512]{1,0:T(8,128)(2,1)S(1)} %broadcast_select_fusion.1.x_ref), channel_id=1, source_target_pairs={{0,4},{1,3},{2,6},{3,1},{4,0},{5,7},{6,2},{7,5},{8,12},{9,11},{10,... | collective-permute-start | bytes 3145736 | tf_op jit(solution)/shard_map/ppermute | solution.py:70
  306.2 42.7 %collective-permute-start.22 = (bf16[1024,512]{1,0:T(8,128)(2,1)S(1)}, bf16[1024,512]{1,0:T(8,128)(2,1)S(1)}, u32[]{:S(2)}, u32[]{:S(2)}) collective-permute-start(bf16[1024,512]{1,0:T(8,128)(2,1)S(1)} %get-tuple-element.29.x_ref), channel_id=1, source_target_pairs={{0,4},{1,3},{2,6},{3,1},{4,0},{5,7},{6,2},{7,5},{8,12},{9,11},{10,... | collective-permute-start | bytes 3145736 | tf_op jit(solution)/shard_map/ppermute | solution.py:70
  351.9 10.3 %collective-permute-start.27 = (f32[160,512]{1,0:T(8,128)S(1)}, f32[160,512]{1,0:T(8,128)S(1)}, u32[]{:S(2)}, u32[]{:S(2)}) collective-permute-start(f32[160,512]{1,0:T(8,128)S(1)} %get-tuple-element.27), channel_id=1, source_target_pairs={{0,2},{1,5},{2,0},{3,7},{4,6},{5,1},{6,4},{7,3},{8,10},{9,13},{10,... | collective-permute-start | bytes 983048 | tf_op jit(solution)/shard_map/ppermute | solution.py:70
  (14 other events, 48.0 us)

commit v2 on v0

--- a/solution.py
+++ b/solution.py
@@ -1,9 +1,17 @@
+import functools
 import math
 
 import jax
 import jax.numpy as jnp
 from jax import lax
+from jax.experimental import pallas as pl
+from jax.experimental.pallas import tpu as pltpu
 from jax.sharding import PartitionSpec as P
+
+AXES = ("donor", "gene")
+HI = lax.Precision.HIGHEST
+VMEM_BYTES = 48 * 1024 * 1024
+FACTOR_BYTES = 1
 
 
 def solve_both(lower_factor, right_cols):
@@ -13,7 +21,7 @@
     )
 
 
-def shards(embeddings, targets_by_gene, cell_counts):
+def shards_any_mesh(embeddings, targets_by_gene, cell_counts):
     valid_count = cell_counts[0]
     gathered = lax.all_gather(embeddings, "gene", axis=1, tiled=True)
     row_total = gathered.shape[0]
@@ -36,8 +44,444 @@
     return lax.dynamic_slice_in_dim(scaled, first_row, share, 0)
 
 
+def permutation(target):
+    pairs = []
+    for z in range(4):
+        for y in range(2):
+            for x in range(2):
+                for c in range(2):
+                    there = target(z, y, x, c)
+                    if there is not None:
+                        tz, ty, tx, tc = there
+                        pairs.append((((z * 2 + y) * 2 + x) * 2 + c, ((tz * 2 + ty) * 2 + tx) * 2 + tc))
+    return pairs
+
+
+CORE = permutation(lambda z, y, x, c: (z, y, x, 1 - c))
+NEAR = permutation(lambda z, y, x, c: (z, y, 1 - x, c) if c == 0 else (z, 1 - y, x, c))
+FAR = permutation(lambda z, y, x, c: (z, 1 - y, x, c) if c == 0 else (z, y, 1 - x, c))
+DIAG_OUT = permutation(lambda z, y, x, c: (z, 1 - y, x, 1) if c == 0 else (z, y, 1 - x, 0))
+DIAG_BACK = permutation(lambda z, y, x, c: (z, y, 1 - x, 1) if c == 0 else (z, 1 - y, x, 0))
+PLANE = [permutation(lambda z, y, x, c, s=s: (z, y ^ (s >> 1), x ^ (s & 1), c)) for s in (1, 2, 3)]
+LINE = [permutation(lambda z, y, x, c, s=s: (z ^ s, y, x, c)) for s in (1, 2, 3)]
+
+MIDDLE = permutation(lambda z, y, x, c: (3 - z, y, x, c) if z in (1, 2) else None)
+OUTWARD = permutation(lambda z, y, x, c: (z ^ 1, y, x, c) if z in (1, 2) else None)
+
+
+def send(value, perm):
+    return lax.ppermute(value, AXES, perm)
+
+
+def pick_kernel(first_row, index_ref, t_ref, *rest):
+    o_ref, held, in_sems, out_sems = rest[-4:]
+    count, rows, block_cells = held.shape
+    copies = []
+    for k in range(count):
+        start = pl.multiple_of(index_ref[k] * block_cells, block_cells)
+        copies.append(
+            (
+                pltpu.make_async_copy(t_ref.at[first_row : first_row + rows, pl.ds(start, block_cells)], held.at[k], in_sems.at[k]),
+                pltpu.make_async_copy(held.at[k], o_ref.at[k], out_sems.at[k]),
+            )
+        )
+    for inward, _ in copies:
+        inward.start()
+    for inward, outward in copies:
+        inward.wait()
+        outward.start()
+    for _, outward in copies:
+        outward.wait()
+
+
+def pick_blocks(targets, block_index, block_cells, after=(), first_row=0, rows=None):
+    rows = rows or targets.shape[0]
+    count = block_index.shape[0]
+    return pl.pallas_call(
+        functools.partial(pick_kernel, first_row),
+        out_shape=jax.ShapeDtypeStruct((count, rows, block_cells), targets.dtype),
+        in_specs=[pl.BlockSpec(memory_space=pltpu.SMEM)]
+        + [pl.BlockSpec(memory_space=pl.ANY)] * (1 + len(after)),
+        out_specs=pl.BlockSpec(memory_space=pl.ANY),
+        scratch_shapes=[
+            pltpu.VMEM((count, rows, block_cells), targets.dtype),
+            pltpu.SemaphoreType.DMA((count,)),
+            pltpu.SemaphoreType.DMA((count,)),
+        ],
+        compiler_params=pltpu.CompilerParams(vmem_limit_bytes=VMEM_BYTES),
+        cost_estimate=pl.CostEstimate(flops=1, bytes_accessed=1, transcendentals=0),
+        name="pick_blocks",
+    )(block_index, targets, *after)
+
+
+def cross_kernel(has_prior, blocks, index_ref, *refs):
+    outs = refs[-4:]
+    prior = refs[6 * blocks : 6 * blocks + 4]
+    rows = outs[0].shape[0]
+    for q in range(4):
+        for first in (0, rows // 2) if q == 2 else (0,):
+            total = None
+            for n in range(blocks):
+                own, from_core, near_low, near_high, from_diag, x_ref = refs[6 * n : 6 * n + 6]
+                piece = (own[...], from_core[0], near_high[0] if first else near_low[0], from_diag[0])[q]
+                part = jnp.dot(piece, x_ref[...], preferred_element_type=jnp.float32)
+                total = part if total is None else total + part
+            place = pl.ds(first, total.shape[0])
+            outs[q][place, :] = total + prior[q][place, :] if has_prior else total
+
+
+def cross_add(prior, targets, received, blocks, after=()):
+    rows = targets.shape[0]
+    whole = lambda shape: pl.BlockSpec(shape, lambda i, index: (0, 0))
+    index, operands, in_specs = [], [], []
+    for n, (block, column, slot, part) in enumerate(blocks):
+        cells, width = block.shape
+        index += [column, slot]
+        operands += [targets, *received, block]
+        in_specs += [pl.BlockSpec((rows, cells), lambda i, index, n=n: (0, index[2 * n]))]
+        in_specs += [
+            pl.BlockSpec((1, value.shape[1], cells), lambda i, index, n=n, part=part: (index[2 * n + 1], 0, part))
+            for value in received
+        ]
+        in_specs += [whole((cells, width))]
+    sums = [whole((rows, width))] * 4
+    aliases = {1 + len(operands) + q: q for q in range(4)} if prior else {}
+    return pl.pallas_call(
+        functools.partial(cross_kernel, prior is not None, len(blocks)),
+        out_shape=[jax.ShapeDtypeStruct((rows, width), jnp.float32)] * 4,
+        grid_spec=pltpu.PrefetchScalarGridSpec(
+            num_scalar_prefetch=1,
+            grid=(1,),
+            in_specs=in_specs + (sums if prior else []) + [pl.BlockSpec(memory_space=pl.ANY)] * len(after),
+            out_specs=sums,
+        ),
+        input_output_aliases=aliases,
+        compiler_params=pltpu.CompilerParams(vmem_limit_bytes=VMEM_BYTES),
+        cost_estimate=pl.CostEstimate(flops=1, bytes_accessed=1, transcendentals=0),
+        name="cross_add",
+    )(jnp.stack(index).astype(jnp.int32), *operands, *(prior or ()), *after)
+
+
+TILE = 128
+SUB = 8
+
+
+def inverse_root(value):
+    root = lax.rsqrt(value)
+    return root * (1.5 - 0.5 * value * root * root)
+
+
+def factor_tiles(tiles):
+    lane = lax.broadcasted_iota(jnp.int32, (SUB, TILE), 1)
+    sub = lax.broadcasted_iota(jnp.int32, (SUB, TILE), 0)
+    wide = lambda value: jnp.broadcast_to(value, (SUB, TILE))
+    count = len(tiles)
+    for p in range(count):
+        low = p * SUB
+        rows = tiles[p]
+        cols = [wide(rows[:, low + k : low + k + 1]) for k in range(SUB)]
+        inside = (lane >= low) & (lane < low + SUB)
+        rows = jnp.where(inside, jnp.where(lane - low == sub, 1.0, 0.0), rows)
+        for k in range(SUB):
+            root = inverse_root(wide(cols[k][k : k + 1, :]))
+            scaled = cols[k] * root
+            for j in range(k + 1, SUB):
+                cols[j] = cols[j] - scaled * wide(scaled[j : j + 1, :])
+            pivot_row = wide(rows[k : k + 1, :]) * root
+            rows = jnp.where(sub == k, pivot_row, jnp.where(sub > k, rows - scaled * pivot_row, rows))
+        tiles[p] = rows
+        if p + 1 < count:
+            right = jnp.where(lane >= low + SUB, rows, 0.0)
+            change = lax.dot_general(
+                right, rows, (((0,), (0,)), ((), ())), precision=HI, preferred_element_type=jnp.float32
+            )
+            for i in range(p + 1, count):
+                tiles[i] = jnp.where(inside, 0.0, tiles[i]) - change[i * SUB : (i + 1) * SUB, :]
+    return jnp.concatenate(tiles, axis=0)
+
+
+def factor_kernel(step, count, v_ref, o_ref):
+    here = slice(step * TILE, (step + 1) * TILE)
+    o_ref[...] = v_ref[...]
+    inverse = factor_tiles([v_ref[step * TILE + i * SUB : step * TILE + (i + 1) * SUB, here] for i in range(TILE // SUB)])
+    down = lax.broadcasted_iota(jnp.int32, (TILE, TILE), 0)
+    across = lax.broadcasted_iota(jnp.int32, (TILE, TILE), 1)
+    inverse = jnp.where(down >= across, inverse, 0.0)
+    o_ref[here, :] = jnp.dot(inverse, v_ref[here, :], precision=HI, preferred_element_type=jnp.float32)
+    o_ref[here, here] = inverse
+    if step + 1 < count:
+        below = slice((step + 1) * TILE, count * TILE)
+        o_ref[below, here] = jnp.zeros((TILE * (count - step - 1), TILE), jnp.float32)
+        o_ref[below, :] = o_ref[below, :] - lax.dot_general(
+            o_ref[here, below], o_ref[here, :], (((0,), (0,)), ((), ())), precision=HI, preferred_element_type=jnp.float32
+        )
+
+
+ANYWHERE = pl.BlockSpec(memory_space=pl.ANY)
+SCALARS = pl.BlockSpec(memory_space=pltpu.SMEM)
+VECTORS = pl.BlockSpec(memory_space=pltpu.VMEM)
+
+
+def small_kernel(body, name, scalars, values, out_shape, after=(), moved=1):
+    def kernel(*refs):
+        given = len(scalars) + len(values)
+        body(refs[:given], refs[given + len(after) :])
+
+    return pl.pallas_call(
+        kernel,
+        out_shape=out_shape,
+        in_specs=[SCALARS] * len(scalars) + [VECTORS] * len(values) + [ANYWHERE] * len(after),
+        compiler_params=pltpu.CompilerParams(vmem_limit_bytes=VMEM_BYTES),
+        cost_estimate=pl.CostEstimate(flops=1, bytes_accessed=moved, transcendentals=0),
+        name=name,
+    )(*scalars, *values, *after)
+
+
+def f32(*shape):
+    return jax.ShapeDtypeStruct(shape, jnp.float32)
+
+
+def gram_rows(which, block, after=()):
+    cells, width = block.shape
+    half = width // 2
+
+    def body(given, outs):
+        which_ref, x_ref = given
+        columns = x_ref[:, pl.ds(pl.multiple_of(which_ref[0] * half, half), half)]
+        outs[0][...] = lax.dot_general(
+            columns, x_ref[...], (((0,), (0,)), ((), ())), preferred_element_type=jnp.float32
+        )
+
+    return small_kernel(body, "gram_rows", [which], [block], f32(half, width), after)
+
+
+def add_split(order, parts, after=()):
+    rows, width = parts[0].shape
+    count = order.shape[0]
+    share = rows // count
+
+    def body(given, outs):
+        order_ref, part_refs = given[0], given[1:]
+        for k in range(count):
+            place = pl.ds(pl.multiple_of(order_ref[k] * share, share), share)
+            total = part_refs[0][place, :]
+            for ref in part_refs[1:]:
+                total = total + ref[place, :]
+            outs[k][...] = total
+
+    return small_kernel(body, "add_split", [order], parts, [f32(share, width)] * count, after)
+
+
+def add_all(parts, after=()):
+    def body(given, outs):
+        total = given[0][...]
+        for ref in given[1:]:
+            total = total + ref[...]
+        outs[0][...] = total
+
+    return small_kernel(body, "add_all", [], parts, f32(*parts[0].shape), after)
+
+
+def place_parts(order, parts, after=()):
+    share, width = parts[0].shape
+    count = len(parts)
+
+    def body(given, outs):
+        for k in range(count):
+            outs[0][pl.ds(pl.multiple_of(given[0][k] * share, share), share), :] = given[1 + k][...]
+
+    return small_kernel(body, "place_parts", [order], parts, f32(share * count, width), after)
+
+
+def copy_rows(value, pieces, after):
+    def body(given, outs):
+        for (first, count), out in zip(pieces, outs):
+            out[...] = given[0][first : first + count, :]
+
+    shapes = [jax.ShapeDtypeStruct((count, value.shape[1]), value.dtype) for _, count in pieces]
+    return small_kernel(body, "copy_rows", [], [value], shapes, after)
+
+
+def live_halves(which, cell_counts, embeddings):
+    slots, width = embeddings.shape
+    half = slots // 2
+
+    def body(given, outs):
+        which_ref, count_ref, x_ref = given
+        for out, part in zip(outs, (which_ref[0], 1 - which_ref[0])):
+            first = pl.multiple_of(part * half, half)
+            row = first + lax.broadcasted_iota(jnp.int32, (half, width), 0)
+            values = x_ref[pl.ds(first, half), :]
+            out[...] = jnp.where(row < count_ref[0], values.astype(jnp.float32), 0.0).astype(values.dtype)
+
+    shape = jax.ShapeDtypeStruct((half, width), embeddings.dtype)
+    return small_kernel(body, "live_halves", [which, cell_counts], [embeddings], [shape] * 2)
+
+
+def join_features(which, mine, other):
+    rows, width = mine.shape
+
+    def body(given, outs):
+        which_ref, mine_ref, other_ref = given
+        first = which_ref[0] == 0
+        values = mine_ref[...], other_ref[...]
+        outs[0][:, :width] = jnp.where(first, values[0], values[1])
+        outs[0][:, width:] = jnp.where(first, values[1], values[0])
+
+    return small_kernel(
+        body, "join_features", [which], [mine, other], jax.ShapeDtypeStruct((rows, 2 * width), mine.dtype)
+    )
+
+
+def choose(which, zero, one, after=()):
+    def body(given, outs):
+        outs[0][...] = jnp.where(given[0][0] == 1, given[2][...], given[1][...])
+
+    return small_kernel(
+        body, "choose", [which], [zero, one], jax.ShapeDtypeStruct(zero.shape, zero.dtype), after
+    )
+
+
+def factor_step(step, value, after=()):
+    width = value.shape[0]
+    body = lambda given, outs: factor_kernel(step, width // TILE, given[0], outs[0])
+    return small_kernel(body, "factor_step", [], [value], f32(width, width), after, moved=FACTOR_BYTES)
+
+
+def gram_inverse(value, scale, after=()):
+    width = value.shape[0]
+
+    def body(given, outs):
+        down = lax.broadcasted_iota(jnp.int32, (width, width), 0)
+        across = lax.broadcasted_iota(jnp.int32, (width, width), 1)
+        lower = jnp.where(down >= across, given[0][...], 0.0)
+        outs[0][...] = scale * lax.dot_general(
+            lower, lower, (((0,), (0,)), ((), ())), precision=HI, preferred_element_type=jnp.float32
+        )
+
+    return small_kernel(body, "gram_inverse", [], [value], f32(width, width), after)
+
+
+def apply_inverse(inverse, parts):
+    width = inverse.shape[0]
+    rows = parts[0].shape[0]
+
+    def body(given, outs):
+        cross = (given[1][...] + given[2][...]) + (given[3][...] + given[4][...])
+        outs[0][...] = lax.dot_general(
+            given[0][...], cross, (((1,), (1,)), ((), ())), precision=HI, preferred_element_type=jnp.float32
+        )
+
+    return small_kernel(body, "apply_inverse", [], [inverse, *parts], f32(width, rows))
+
+
+def shards(embeddings, targets_by_gene, cell_counts):
+    slots = embeddings.shape[0]
+    donors = lax.axis_size("donor")
+    donor = lax.axis_index("donor")
+    c = lax.axis_index("gene")
+    z, y, x = donor // 4, (donor // 2) % 2, donor % 2
+    near_bit = jnp.where(c == 0, x, y)
+    far_bit = jnp.where(c == 0, y, x)
+    half = slots // 2
+    ints = lambda *values: jnp.stack(values).astype(jnp.int32)
+
+    def group_donor(k, core, bit):
+        line, other = k // 2, k % 2
+        return line * 4 + jnp.where(core == 0, other * 2 + bit, bit * 2 + other)
+
+    ks = jnp.arange(8, dtype=jnp.int32)
+
+    def blocks_for(core, bit):
+        return (group_donor(ks, core, bit) * 2 + core).astype(jnp.int32)
+
+    core = ints(c)
+    keep, give = live_halves(core, cell_counts, embeddings)
+    got = send(give, CORE)
+    block = join_features(core, keep, got)
+    rows = targets_by_gene.shape[0]
+    line1 = send(block, LINE[0])
+    far_own = send(block, FAR)
+
+    gram_give = gram_rows(ints(1 - c), block)
+    gram_got = send(gram_give, CORE)
+    gram_keep = gram_rows(ints(c), block, after=(gram_give,))
+    place = donor % 4
+    order = ints(place, place ^ 1, place ^ 2, place ^ 3)
+    mine, *others = add_split(order, [gram_keep, gram_got])
+    parts = [mine] + [send(other, PLANE[s]) for s, other in enumerate(others)]
+    plane_sum = add_all(parts, after=(far_own,))
+    near_low = pick_blocks(targets_by_gene, blocks_for(c, 1 - near_bit), half, (plane_sum,), 0, rows // 2)
+    near_low = send(near_low, NEAR)
+
+    line_parts = [plane_sum] + [send(plane_sum, LINE[s]) for s in range(3)]
+    total = add_all(line_parts, after=(line1,))
+
+    quarters = [total] + [send(total, PLANE[s]) for s in range(3)]
+    (late,) = copy_rows(block, ((0, half),), (total,))
+    middle_own = send(late, MIDDLE)
+    quarter = place_parts(order, quarters, (late,))
+    (late,) = copy_rows(line1, ((0, half),), (quarter,))
+    middle_outer = send(late, MIDDLE)
+    near_high = pick_blocks(
+        targets_by_gene, blocks_for(c, 1 - near_bit), half, (late,), rows // 2, rows // 2
+    )
+    gram = place_parts(ints(c, 1 - c), [quarter, send(quarter, CORE)], after=(near_high, near_low))
+    near_high = send(near_high, NEAR)
+    value = factor_step(0, gram)
+    for_diag = pick_blocks(targets_by_gene, blocks_for(1 - c, 1 - far_bit), half, (value,))
+    from_diag = send(for_diag, DIAG_OUT)
+    for_core = pick_blocks(targets_by_gene, blocks_for(1 - c, far_bit), half, after=(for_diag,))
+    from_core = send(for_core, CORE)
+
+    value = factor_step(1, value, after=(for_core,))
+    (late,) = copy_rows(middle_own, ((0, half),), (value, near_high))
+    outward_own = send(late, OUTWARD)
+    (late,) = copy_rows(line1, ((0, half),), (late,))
+    far1 = send(late, FAR)
+    value = factor_step(2, value, after=(late,))
+    value = factor_step(3, value)
+    inverse = gram_inverse(value, math.sqrt(slots * donors))
+    (late,) = copy_rows(middle_outer, ((0, half),), (inverse,))
+    outward_outer = send(late, OUTWARD)
+    is_middle = jnp.where((z == 1) | (z == 2), 1, 0)
+    second = choose(ints(is_middle), outward_own, middle_own, (late,))
+    far2 = send(second, FAR)
+    third = choose(ints(is_middle), outward_outer, middle_outer)
+    far3 = send(third, FAR)
+    second_z = jnp.where(is_middle == 1, z ^ 3, z ^ 2)
+    third_z = jnp.where(is_middle == 1, z ^ 2, z ^ 3)
+
+    def cells_of(piece, cells_z, other, part=0):
+        k = cells_z * 2 + other
+        column = (group_donor(k, c, near_bit) * 2 + c) * (half // piece.shape[0]) + part
+        return piece, column, k, part
+
+    received = (from_core, near_low, near_high, from_diag)
+    acc = None
+    for blocks in (
+        [(block, z, far_bit), (far_own, z, 1 - far_bit), (line1, z ^ 1, far_bit)],
+        [(second, second_z, far_bit), (far1, z ^ 1, 1 - far_bit)],
+        [(third, third_z, far_bit), (far2, second_z, 1 - far_bit)],
+        [(far3, third_z, 1 - far_bit)],
+    ):
+        acc = cross_add(
+            acc, targets_by_gene, received, [cells_of(*block) for block in blocks], (inverse,) if acc is None else ()
+        )
+    own, for_other, to_near, to_diag = acc
+    scaled = apply_inverse(
+        inverse, [own, send(for_other, CORE), send(to_near, NEAR), send(to_diag, DIAG_BACK)]
+    )
+    return lax.all_to_all(scaled, "donor", split_axis=0, concat_axis=1, tiled=True)
+
+
 def solution(mesh):
     placed = (P("donor", "gene"), P(("gene", "donor"), None), P("donor"))
+    tuned = mesh.shape["donor"] == 16 and mesh.shape["gene"] == 2
     return jax.shard_map(
-        shards, mesh=mesh, in_specs=placed, out_specs=P("donor", "gene"), check_vma=False
-    )
+        shards if tuned else shards_any_mesh,
+        mesh=mesh,
+        in_specs=placed,
+        out_specs=P("donor", "gene"),
+        check_vma=False,
+    )

time: 659 us -> 206 us (0.31)
  waiting for transfers between devices: 443 us -> 56.9 us
  other arithmetic: 120 us -> 0.41 us
  Pallas kernels: 0 us -> 88.3 us
  matrix products: 41.6 us -> 0 us
  starting transfers between devices: 8.44 us -> 32.8 us
  blocking collectives: 0 us -> 19.9 us
  local copies, waits for them, and re-layouts: 22.4 us -> 6.22 us
  between operations: 17.2 us -> 1.06 us
    psum x1 -> x0, waiting for transfers between devices: 252 us -> none  [shards(): cross_sum = lax.psum(cross_local, 'donor')]
    all_to_all x1 -> x0, waiting for transfers between devices: 178 us -> none  [shards(): lax.all_to_all(targets_by_gene, 'donor', split_axis=1, concat_axis=0, til...]
    another operation x17 -> x5, other arithmetic: 119 us -> 0.38 us  [the longest x3 0.23 us: cross_add(): jnp.stack(index).astype(jnp.int32)]
    pallas_call x0 -> x30, Pallas kernels: none -> 88.3 us  [the longest x22 58.2 us: small_kernel(): pl.pallas_call(kernel, out_shape=out_shape, in_specs=[SCALARS] * len(scal...]
    ppermute x0 -> x28, waiting for transfers between devices: none -> 56.9 us  [send(): return lax.ppermute(value, AXES, perm)]
    ppermute x0 -> x28, starting transfers between devices: none -> 32.8 us  [send(): return lax.ppermute(value, AXES, perm)]
    another operation x20 -> x0, matrix products: 25.6 us -> none  [the longest x7 13.1 us: solve_both(): lax.linalg.triangular_solve(lower_factor, right_cols, left_side=True, low...]
    all_to_all x0 -> x1, blocking collectives: none -> 19.9 us  [shards(): lax.all_to_all(scaled, 'donor', split_axis=0, concat_axis=1, tiled=True)]
  transfers between devices with their start and end apart: 3 -> 28, of which waited for: 3 -> 13; matrix products, arithmetic and copies ran while one was open for 1% -> 0% of each run, Pallas kernels for 0% -> 41%
where the time goes in v2:
time: 206 us
  Pallas kernels  88.3 us (43%)
  waiting for transfers between devices  56.9 us (28%)
  starting transfers between devices  32.8 us (16%)
  blocking collectives  19.9 us (10%)
  local copies, waits for them, and re-layouts  6.22 us (3%)
    pallas_call x22, Pallas kernels, small_kernel(): pl.pallas_call(kernel, out_shape=out_shape, in_specs=[SCALARS] * len(scal...  58.2 us
    ppermute x28, waiting for transfers between devices, send(): return lax.ppermute(value, AXES, perm)  56.9 us
    ppermute x28, starting transfers between devices, send(): return lax.ppermute(value, AXES, perm)  32.8 us
    all_to_all x1, blocking collectives, shards(): lax.all_to_all(scaled, 'donor', split_axis=0, concat_axis=1, tiled=True)  19.9 us
    pallas_call x4, Pallas kernels, cross_add(): pl.pallas_call(functools.partial(cross_kernel, prior is not None, len(blo...  18.1 us
    pallas_call x4, Pallas kernels, pick_blocks(): pl.pallas_call(functools.partial(pick_kernel, first_row), out_shape=jax.S...  12 us
    unnamed x28, local copies, waits for them, and re-layouts  4.84 us
  transfers between devices with their start and end apart: 28, of which 13 were waited for; matrix products, arithmetic and copies ran while one was open for 0% of the time, Pallas kernels for 41%

profile of v2, /device:TPU:0, one launch (start us, length us, event | category | flops | bytes accessed | tf_op | source)
XLA Modules:
  0.0 205.6 jit_solution(16968716965946748892)
XLA Ops:
  4.3 3.0 %collective-permute-start.5 = (bf16[1024,512]{1,0:T(8,128)(2,1)S(1)}, bf16[1024,512]{1,0:T(8,128)(2,1)S(1)}, u32[]{:S(2)}, u32[]{:S(2)}) collective-permute-start(bf16[1024,512]{1,0:T(8,128)(2,1)S(1)} %join_features.1.refs_1_.refs_0_.refs_5_), channel_id=1, source_target_pairs={{0,4},{1,3},{2,6},{3,1},{4,0},{5,7},{6,2},{7,5},{8,12},{9,11},{10,... | collective-permute-start | bytes 3145736 | tf_op jit(solution)/shard_map/ppermute | solution.py:73
  16.1 3.1 %collective-permute-done.2.refs_1_ = f32[64,512]{1,0:T(8,128)S(1)} collective-permute-done((f32[64,512]{1,0:T(8,128)}, f32[64,512]{1,0:T(8,128)S(1)}, u32[]{:S(2)}, u32[]{:S(2)}) %collective-permute-start.2) | collective-permute-done | bytes 131104 | tf_op jit(solution)/shard_map/ppermute | solution.py:73
  19.3 6.0 %collective-permute-done.3.refs_2_ = f32[64,512]{1,0:T(8,128)S(1)} collective-permute-done((f32[64,512]{1,0:T(8,128)}, f32[64,512]{1,0:T(8,128)S(1)}, u32[]{:S(2)}, u32[]{:S(2)}) %collective-permute-start.3) | collective-permute-done | bytes 131104 | tf_op jit(solution)/shard_map/ppermute | solution.py:73
  26.4 2.8 %pick_blocks.5 = bf16[8,80,1024]{2,1,0:T(8,128)(2,1)} custom-call(s32[8]{0:T(128)S(1)} %fusion.9.index_ref, bf16[160,32768]{1,0:T(8,128)(2,1)} %refs_0_.7, f32[64,512]{1,0:T(8,128)S(1)} %add_all.2.refs_0_.rest_0_), custom_call_target="tpu_custom_call" | custom-call | flops 1 | bytes 1 | tf_op jit(solution)/shard_map/pick_blocks/pallas_call | solution.py:100
  32.3 2.6 %collective-permute-start.7 = (f32[64,512]{1,0:T(8,128)S(1)}, f32[64,512]{1,0:T(8,128)S(1)}, u32[]{:S(2)}, u32[]{:S(2)}) collective-permute-start(f32[64,512]{1,0:T(8,128)S(1)} %add_all.2.refs_0_.rest_0_), channel_id=1, source_target_pairs={{0,16},{1,17},{2,18},{3,19},{4,20},{5,21},{6,22},{7,23},{8,24},{9,... | collective-permute-start | bytes 393224 | tf_op jit(solution)/shard_map/ppermute | solution.py:73
  35.1 4.3 %collective-permute-done.6.refs_1_ = f32[64,512]{1,0:T(8,128)S(1)} collective-permute-done((f32[64,512]{1,0:T(8,128)S(1)}, f32[64,512]{1,0:T(8,128)S(1)}, u32[]{:S(2)}, u32[]{:S(2)}) %collective-permute-start.6) | collective-permute-done | bytes 131104 | tf_op jit(solution)/shard_map/ppermute | solution.py:73
  39.5 5.7 %collective-permute-done.7.refs_2_ = f32[64,512]{1,0:T(8,128)S(1)} collective-permute-done((f32[64,512]{1,0:T(8,128)S(1)}, f32[64,512]{1,0:T(8,128)S(1)}, u32[]{:S(2)}, u32[]{:S(2)}) %collective-permute-start.7) | collective-permute-done | bytes 131104 | tf_op jit(solution)/shard_map/ppermute | solution.py:73
  56.9 2.8 %pick_blocks.4.refs_3_ = bf16[8,80,1024]{2,1,0:T(8,128)(2,1)} custom-call(s32[8]{0:T(128)S(1)} %fusion.9.index_ref, bf16[160,32768]{1,0:T(8,128)(2,1)} %refs_0_.7, bf16[1024,512]{1,0:T(8,128)(2,1)} %copy_rows.6.rest_0_), custom_call_target="tpu_custom_call" | custom-call | flops 1 | bytes 1 | tf_op jit(solution)/shard_map/pick_blocks/pallas_call | solution.py:100
  68.5 9.1 %factor_step.4.rest_0_.refs_0_ = f32[512,512]{1,0:T(8,128)S(1)} custom-call(f32[512,512]{1,0:T(8,128)S(1)} %copy-done.12), custom_call_target="tpu_custom_call" | custom-call | flops 1 | bytes 1 | tf_op jit(solution)/shard_map/factor_step/pallas_call | solution.py:230
  77.6 3.2 %pick_blocks.6.rest_0_ = bf16[8,160,1024]{2,1,0:T(8,128)(2,1)} custom-call(s32[8]{0:T(128)S(1)} %fusion.7.index_ref, bf16[160,32768]{1,0:T(8,128)(2,1)} %refs_0_.7, f32[512,512]{1,0:T(8,128)S(1)} %factor_step.4.rest_0_.refs_0_), custom_call_target="tpu_custom_call" | custom-call | flops 1 | bytes 1 | tf_op jit(solution)/shard_map/pick_blocks/pallas_call | solution.py:100
  80.8 3.2 %pick_blocks.7.refs_1_ = bf16[8,160,1024]{2,1,0:T(8,128)(2,1)} custom-call(s32[8]{0:T(128)S(1)} %fusion.8.index_ref, bf16[160,32768]{1,0:T(8,128)(2,1)} %refs_0_.7, bf16[8,160,1024]{2,1,0:T(8,128)(2,1)} %pick_blocks.6.rest_0_), custom_call_target="tpu_custom_call" | custom-call | flops 1 | bytes 1 | tf_op jit(solution)/shard_map/pick_blocks/pallas_call | solution.py:100
  84.5 8.9 %factor_step.5.refs_1_.refs_0_ = f32[512,512]{1,0:T(8,128)S(1)} custom-call(f32[512,512]{1,0:T(8,128)S(1)} %factor_step.4.rest_0_.refs_0_, bf16[8,160,1024]{2,1,0:T(8,128)(2,1)} %pick_blocks.7.refs_1_), custom_call_target="tpu_custom_call" | custom-call | flops 1 | bytes 1 | tf_op jit(solution)/shard_map/factor_step/pallas_call | solution.py:230
  97.8 8.6 %factor_step.6.refs_0_ = f32[512,512]{1,0:T(8,128)S(1)} custom-call(f32[512,512]{1,0:T(8,128)S(1)} %factor_step.5.refs_1_.refs_0_, bf16[1024,512]{1,0:T(8,128)(2,1)} %copy_rows.8.refs_1_), custom_call_target="tpu_custom_call" | custom-call | flops 1 | bytes 1 | tf_op jit(solution)/shard_map/factor_step/pallas_call | solution.py:230
  106.5 8.3 %factor_step.7.refs_0_ = f32[512,512]{1,0:T(8,128)S(1)} custom-call(f32[512,512]{1,0:T(8,128)S(1)} %factor_step.6.refs_0_), custom_call_target="tpu_custom_call" | custom-call | flops 1 | bytes 1 | tf_op jit(solution)/shard_map/factor_step/pallas_call | solution.py:230
  124.5 2.6 %choose.3.refs_5_ = bf16[1024,512]{1,0:T(8,128)(2,1)} custom-call(s32[1]{0:T(128)} %bitcast.8.refs_0_, bf16[1024,512]{1,0:T(8,128)(2,1)} %collective-permute-done.22.refs_1_, bf16[1024,512]{1,0:T(8,128)(2,1)} %collective-permute-done.15.refs_0_.refs_2_, bf16[1024,512]{1,0:T(8,128)(2,1)} %copy_rows.9.refs_3_), custom_call_target="tpu_custom_call" | custom-call | flops 1 | bytes 1 | tf_op jit(solution)/shard_map/choose/pallas_call | solution.py:230
  128.6 20.6 %collective-permute-done.20.refs_1_ = bf16[1024,512]{1,0:T(8,128)(2,1)} collective-permute-done((bf16[1024,512]{1,0:T(8,128)(2,1)}, bf16[1024,512]{1,0:T(8,128)(2,1)}, u32[]{:S(2)}, u32[]{:S(2)}) %collective-permute-start.20) | collective-permute-done | bytes 1048608 | tf_op jit(solution)/shard_map/ppermute | solution.py:73
  149.2 2.6 %choose.2.refs_5_ = bf16[1024,512]{1,0:T(8,128)(2,1)} custom-call(s32[1]{0:T(128)} %bitcast.8.refs_0_, bf16[1024,512]{1,0:T(8,128)(2,1)} %collective-permute-done.20.refs_1_, bf16[1024,512]{1,0:T(8,128)(2,1)} %collective-permute-done.19.refs_0_.refs_2_), custom_call_target="tpu_custom_call" | custom-call | flops 1 | bytes 1 | tf_op jit(solution)/shard_map/choose/pallas_call | solution.py:230
  154.9 5.4 %cross_add.4 = (f32[160,512]{1,0:T(8,128)S(1)}, f32[160,512]{1,0:T(8,128)S(1)}, f32[160,512]{1,0:T(8,128)S(1)}, f32[160,512]{1,0:T(8,128)S(1)}) custom-call(s32[6]{0:T(128)S(1)} %stack.119.index_ref, bf16[160,32768]{1,0:T(8,128)(2,1)} %refs_0_.7, bf16[8,160,1024]{2,1,0:T(8,128)(2,1)} %collective-permute-done.17.refs_1_.refs_7_.refs_13_, ...), custom_call_target="tpu_custom_call" | custom-call | flops 1 | bytes 1 | tf_op jit(solution)/shard_map/cross_add/pallas_call | solution.py:149
  160.4 4.7 %cross_add.5 = (f32[160,512]{1,0:T(8,128)S(1)}, f32[160,512]{1,0:T(8,128)S(1)}, f32[160,512]{1,0:T(8,128)S(1)}, f32[160,512]{1,0:T(8,128)S(1)}) custom-call(s32[4]{0:T(128)S(1)} %pad_add_fusion.4.index_ref, bf16[160,32768]{1,0:T(8,128)(2,1)} %refs_0_.7, ...), custom_call_target="tpu_custom_call", output_to_operand_aliasing={{0}: (13, {}), {1}: (14, {}), {2}: (15, {}), {3}: (16, {})} | custom-call | flops 1 | bytes 1 | tf_op jit(solution)/shard_map/cross_add/pallas_call | solution.py:149
  165.2 4.7 %cross_add.6 = (f32[160,512]{1,0:T(8,128)S(1)}, f32[160,512]{1,0:T(8,128)S(1)}, f32[160,512]{1,0:T(8,128)S(1)}, f32[160,512]{1,0:T(8,128)S(1)}) custom-call(s32[4]{0:T(128)S(1)} %pad_add_fusion.3.index_ref, bf16[160,32768]{1,0:T(8,128)(2,1)} %refs_0_.7, ...), custom_call_target="tpu_custom_call", output_to_operand_aliasing={{0}: (13, {}), {1}: (14, {}), {2}: (15, {}), {3}: (16, {})} | custom-call | flops 1 | bytes 1 | tf_op jit(solution)/shard_map/cross_add/pallas_call | solution.py:149
  169.9 3.2 %cross_add.7 = (f32[160,512]{1,0:T(8,128)S(1)}, f32[160,512]{1,0:T(8,128)S(1)}, f32[160,512]{1,0:T(8,128)S(1)}, f32[160,512]{1,0:T(8,128)S(1)}) custom-call(s32[2]{0:T(128)S(1)} %pad_add_fusion.2.index_ref, bf16[160,32768]{1,0:T(8,128)(2,1)} %refs_0_.7, ...), custom_call_target="tpu_custom_call", output_to_operand_aliasing={{0}: (7, {}), {1}: (8, {}), {2}: (9, {}), {3}: (10, {})} | custom-call | flops 1 | bytes 1 | tf_op jit(solution)/shard_map/cross_add/pallas_call | solution.py:149
  174.9 5.5 %collective-permute-done.26.refs_3_ = f32[160,512]{1,0:T(8,128)S(1)} collective-permute-done((f32[160,512]{1,0:T(8,128)S(1)}, f32[160,512]{1,0:T(8,128)S(1)}, u32[]{:S(2)}, u32[]{:S(2)}) %collective-permute-start.26) | collective-permute-done | bytes 327712 | tf_op jit(solution)/shard_map/ppermute | solution.py:73
  180.4 3.0 %collective-permute-done.27.refs_4_ = f32[160,512]{1,0:T(8,128)S(1)} collective-permute-done((f32[160,512]{1,0:T(8,128)S(1)}, f32[160,512]{1,0:T(8,128)S(1)}, u32[]{:S(2)}, u32[]{:S(2)}) %collective-permute-start.27) | collective-permute-done | bytes 327712 | tf_op jit(solution)/shard_map/ppermute | solution.py:73
  184.4 19.9 %all_to_all.19 = f32[16,32,160]{2,1,0:T(8,128)S(1)} all-to-all(f32[16,32,160]{2,1,0:T(8,128)S(1)} %bitcast.25), channel_id=1, replica_groups=mesh['donor'=16,'gene'=2] {'donor'}, dimensions={0} | all-to-all | bytes 655360 | tf_op jit(solution)/shard_map/all_to_all | solution.py:475
  (102 shorter events, 60.7 us)
Async XLA Ops:
  4.3 21.0 %collective-permute-start.5 = (bf16[1024,512]{1,0:T(8,128)(2,1)S(1)}, bf16[1024,512]{1,0:T(8,128)(2,1)S(1)}, u32[]{:S(2)}, u32[]{:S(2)}) collective-permute-start(bf16[1024,512]{1,0:T(8,128)(2,1)S(1)} %join_features.1.refs_1_.refs_0_.refs_5_), channel_id=1, source_target_pairs={{0,4},{1,3},{2,6},{3,1},{4,0},{5,7},{6,2},{7,5},{8,12},{9,11},{10,... | collective-permute-start | bytes 3145736 | tf_op jit(solution)/shard_map/ppermute | solution.py:73
  8.6 26.6 %collective-permute-start.9 = (bf16[1024,512]{1,0:T(8,128)(2,1)S(1)}, bf16[1024,512]{1,0:T(8,128)(2,1)S(1)}, u32[]{:S(2)}, u32[]{:S(2)}) collective-permute-start(bf16[1024,512]{1,0:T(8,128)(2,1)S(1)} %join_features.1.refs_1_.refs_0_.refs_5_), channel_id=1, source_target_pairs={{0,8},{1,9},{2,10},{3,11},{4,12},{5,13},{6,14},{7,15},{8,0},{9,1},... | collective-permute-start | bytes 3145736 | tf_op jit(solution)/shard_map/ppermute | solution.py:73
  12.6 6.6 %collective-permute-start.2 = (f32[64,512]{1,0:T(8,128)}, f32[64,512]{1,0:T(8,128)S(1)}, u32[]{:S(2)}, u32[]{:S(2)}) collective-permute-start(f32[64,512]{1,0:T(8,128)} %get-tuple-element.30), channel_id=1, source_target_pairs={{0,2},{1,3},{2,0},{3,1},{4,6},{5,7},{6,4},{7,5},{8,10},{9,11},{10,... | collective-permute-start | bytes 393224 | tf_op jit(solution)/shard_map/ppermute | solution.py:73
  14.1 11.2 %collective-permute-start.3 = (f32[64,512]{1,0:T(8,128)}, f32[64,512]{1,0:T(8,128)S(1)}, u32[]{:S(2)}, u32[]{:S(2)}) collective-permute-start(f32[64,512]{1,0:T(8,128)} %get-tuple-element.31), channel_id=1, source_target_pairs={{0,4},{1,5},{2,6},{3,7},{4,0},{5,1},{6,2},{7,3},{8,12},{9,13},{10,... | collective-permute-start | bytes 393224 | tf_op jit(solution)/shard_map/ppermute | solution.py:73
  14.6 10.7 %collective-permute-start.4 = (f32[64,512]{1,0:T(8,128)}, f32[64,512]{1,0:T(8,128)}, u32[]{:S(2)}, u32[]{:S(2)}) collective-permute-start(f32[64,512]{1,0:T(8,128)} %get-tuple-element.32), channel_id=1, source_target_pairs={{0,6},{1,7},{2,4},{3,5},{4,2},{5,3},{6,0},{7,1},{8,14},{9,15},{10,... | collective-permute-start | bytes 393224 | tf_op jit(solution)/shard_map/ppermute | solution.py:73
  29.2 35.6 %collective-permute-start.14 = (bf16[8,80,1024]{2,1,0:T(8,128)(2,1)}, bf16[8,80,1024]{2,1,0:T(8,128)(2,1)S(1)}, u32[]{:S(2)}, u32[]{:S(2)}) collective-permute-start(bf16[8,80,1024]{2,1,0:T(8,128)(2,1)} %pick_blocks.5), channel_id=1, source_target_pairs={{0,2},{1,5},{2,0},{3,7},{4,6},{5,1},{6,4},{7,3},{8,10},{9,13},{10,... | collective-permute-start | bytes 3932168 | tf_op jit(solution)/shard_map/ppermute | solution.py:73
  30.7 8.7 %collective-permute-start.6 = (f32[64,512]{1,0:T(8,128)S(1)}, f32[64,512]{1,0:T(8,128)S(1)}, u32[]{:S(2)}, u32[]{:S(2)}) collective-permute-start(f32[64,512]{1,0:T(8,128)S(1)} %add_all.2.refs_0_.rest_0_), channel_id=1, source_target_pairs={{0,8},{1,9},{2,10},{3,11},{4,12},{5,13},{6,14},{7,15},{8,0},{9,1},... | collective-permute-start | bytes 393224 | tf_op jit(solution)/shard_map/ppermute | solution.py:73
  32.3 12.8 %collective-permute-start.7 = (f32[64,512]{1,0:T(8,128)S(1)}, f32[64,512]{1,0:T(8,128)S(1)}, u32[]{:S(2)}, u32[]{:S(2)}) collective-permute-start(f32[64,512]{1,0:T(8,128)S(1)} %add_all.2.refs_0_.rest_0_), channel_id=1, source_target_pairs={{0,16},{1,17},{2,18},{3,19},{4,20},{5,21},{6,22},{7,23},{8,24},{9,... | collective-permute-start | bytes 393224 | tf_op jit(solution)/shard_map/ppermute | solution.py:73
  34.9 10.2 %collective-permute-start.8 = (f32[64,512]{1,0:T(8,128)S(1)}, f32[64,512]{1,0:T(8,128)S(1)}, u32[]{:S(2)}, u32[]{:S(2)}) collective-permute-start(f32[64,512]{1,0:T(8,128)S(1)} %add_all.2.refs_0_.rest_0_), channel_id=1, source_target_pairs={{0,24},{1,25},{2,26},{3,27},{4,28},{5,29},{6,30},{7,31},{8,16},{9,... | collective-permute-start | bytes 393224 | tf_op jit(solution)/shard_map/ppermute | solution.py:73
  45.2 5.9 %collective-permute-start.10 = (f32[64,512]{1,0:T(8,128)S(1)}, f32[64,512]{1,0:T(8,128)S(1)}, u32[]{:S(2)}, u32[]{:S(2)}) collective-permute-start(f32[64,512]{1,0:T(8,128)S(1)} %add_all.3.refs_1_), channel_id=1, source_target_pairs={{0,2},{1,3},{2,0},{3,1},{4,6},{5,7},{6,4},{7,5},{8,10},{9,11},{10,... | collective-permute-start | bytes 393224 | tf_op jit(solution)/shard_map/ppermute | solution.py:73
  46.3 6.7 %collective-permute-start.11 = (f32[64,512]{1,0:T(8,128)S(1)}, f32[64,512]{1,0:T(8,128)S(1)}, u32[]{:S(2)}, u32[]{:S(2)}) collective-permute-start(f32[64,512]{1,0:T(8,128)S(1)} %add_all.3.refs_1_), channel_id=1, source_target_pairs={{0,4},{1,5},{2,6},{3,7},{4,0},{5,1},{6,2},{7,3},{8,12},{9,13},{10,... | collective-permute-start | bytes 393224 | tf_op jit(solution)/shard_map/ppermute | solution.py:73
  48.1 6.3 %collective-permute-start.12 = (f32[64,512]{1,0:T(8,128)S(1)}, f32[64,512]{1,0:T(8,128)S(1)}, u32[]{:S(2)}, u32[]{:S(2)}) collective-permute-start(f32[64,512]{1,0:T(8,128)S(1)} %add_all.3.refs_1_), channel_id=1, source_target_pairs={{0,6},{1,7},{2,4},{3,5},{4,2},{5,3},{6,0},{7,1},{8,14},{9,15},{10,... | collective-permute-start | bytes 393224 | tf_op jit(solution)/shard_map/ppermute | solution.py:73
  59.7 33.7 %collective-permute-start.16 = (bf16[8,80,1024]{2,1,0:T(8,128)(2,1)}, bf16[8,80,1024]{2,1,0:T(8,128)(2,1)S(1)}, u32[]{:S(2)}, u32[]{:S(2)}) collective-permute-start(bf16[8,80,1024]{2,1,0:T(8,128)(2,1)} %pick_blocks.4.refs_3_), channel_id=1, source_target_pairs={{0,2},{1,5},{2,0},{3,7},{4,6},{5,1},{6,4},{7,3},{8,10},{9,13},{10,... | collective-permute-start | bytes 3932168 | tf_op jit(solution)/shard_map/ppermute | solution.py:73
  61.3 32.1 %collective-permute-start.15 = (bf16[1024,512]{1,0:T(8,128)(2,1)}, bf16[1024,512]{1,0:T(8,128)(2,1)}, u32[]{:S(2)}, u32[]{:S(2)}) collective-permute-start(bf16[1024,512]{1,0:T(8,128)(2,1)} %copy_rows.5.refs_5_), channel_id=1, source_target_pairs={{8,16},{9,17},{10,18},{11,19},{12,20},{13,21},{14,22},{15,23},{16,... | collective-permute-start | bytes 3145736 | tf_op jit(solution)/shard_map/ppermute | solution.py:73
  63.0 53.6 %collective-permute-start.19 = (bf16[1024,512]{1,0:T(8,128)(2,1)}, bf16[1024,512]{1,0:T(8,128)(2,1)}, u32[]{:S(2)}, u32[]{:S(2)}) collective-permute-start(bf16[1024,512]{1,0:T(8,128)(2,1)} %copy_rows.6.rest_0_), channel_id=1, source_target_pairs={{8,16},{9,17},{10,18},{11,19},{12,20},{13,21},{14,22},{15,23},{16,... | collective-permute-start | bytes 3145736 | tf_op jit(solution)/shard_map/ppermute | solution.py:73
  84.0 69.5 %collective-permute-start.17 = (bf16[8,160,1024]{2,1,0:T(8,128)(2,1)}, bf16[8,160,1024]{2,1,0:T(8,128)(2,1)}, u32[]{:S(2)}, u32[]{:S(2)}) collective-permute-start(bf16[8,160,1024]{2,1,0:T(8,128)(2,1)} %pick_blocks.7.refs_1_), channel_id=1, source_target_pairs={{0,1},{1,0},{2,3},{3,2},{4,5},{5,4},{6,7},{7,6},{8,9},{9,8},{10,11... | collective-permute-start | bytes 7864328 | tf_op jit(solution)/shard_map/ppermute | solution.py:73
  84.5 69.0 %collective-permute-start.18 = (bf16[8,160,1024]{2,1,0:T(8,128)(2,1)}, bf16[8,160,1024]{2,1,0:T(8,128)(2,1)}, u32[]{:S(2)}, u32[]{:S(2)}) collective-permute-start(bf16[8,160,1024]{2,1,0:T(8,128)(2,1)} %pick_blocks.6.rest_0_), channel_id=1, source_target_pairs={{0,5},{1,2},{2,7},{3,0},{4,1},{5,6},{6,3},{7,4},{8,13},{9,10},{10,... | collective-permute-start | bytes 7864328 | tf_op jit(solution)/shard_map/ppermute | solution.py:73
  95.3 29.2 %collective-permute-start.22 = (bf16[1024,512]{1,0:T(8,128)(2,1)S(1)}, bf16[1024,512]{1,0:T(8,128)(2,1)}, u32[]{:S(2)}, u32[]{:S(2)}) collective-permute-start(bf16[1024,512]{1,0:T(8,128)(2,1)S(1)} %copy_rows.7.refs_1_), channel_id=1, source_target_pairs={{8,0},{9,1},{10,2},{11,3},{12,4},{13,5},{14,6},{15,7},{16,24},{17,... | collective-permute-start | bytes 3145736 | tf_op jit(solution)/shard_map/ppermute | solution.py:73
  118.9 30.3 %collective-permute-start.20 = (bf16[1024,512]{1,0:T(8,128)(2,1)}, bf16[1024,512]{1,0:T(8,128)(2,1)}, u32[]{:S(2)}, u32[]{:S(2)}) collective-permute-start(bf16[1024,512]{1,0:T(8,128)(2,1)} %copy_rows.9.refs_3_), channel_id=1, source_target_pairs={{8,0},{9,1},{10,2},{11,3},{12,4},{13,5},{14,6},{15,7},{16,24},{17,... | collective-permute-start | bytes 3145736 | tf_op jit(solution)/shard_map/ppermute | solution.py:73
  120.4 40.0 %collective-permute-start.24 = (bf16[1024,512]{1,0:T(8,128)(2,1)}, bf16[1024,512]{1,0:T(8,128)(2,1)}, u32[]{:S(2)}, u32[]{:S(2)}) collective-permute-start(bf16[1024,512]{1,0:T(8,128)(2,1)} %copy_rows.8.refs_1_), channel_id=1, source_target_pairs={{0,4},{1,3},{2,6},{3,1},{4,0},{5,7},{6,2},{7,5},{8,12},{9,11},{10,... | collective-permute-start | bytes 3145736 | tf_op jit(solution)/shard_map/ppermute | solution.py:73
  127.2 38.0 %collective-permute-start.23 = (bf16[1024,512]{1,0:T(8,128)(2,1)}, bf16[1024,512]{1,0:T(8,128)(2,1)}, u32[]{:S(2)}, u32[]{:S(2)}) collective-permute-start(bf16[1024,512]{1,0:T(8,128)(2,1)} %choose.3.refs_5_), channel_id=1, source_target_pairs={{0,4},{1,3},{2,6},{3,1},{4,0},{5,7},{6,2},{7,5},{8,12},{9,11},{10,... | collective-permute-start | bytes 3145736 | tf_op jit(solution)/shard_map/ppermute | solution.py:73
  151.8 18.1 %collective-permute-start.21 = (bf16[1024,512]{1,0:T(8,128)(2,1)}, bf16[1024,512]{1,0:T(8,128)(2,1)}, u32[]{:S(2)}, u32[]{:S(2)}) collective-permute-start(bf16[1024,512]{1,0:T(8,128)(2,1)} %choose.2.refs_5_), channel_id=1, source_target_pairs={{0,4},{1,3},{2,6},{3,1},{4,0},{5,7},{6,2},{7,5},{8,12},{9,11},{10,... | collective-permute-start | bytes 3145736 | tf_op jit(solution)/shard_map/ppermute | solution.py:73
  173.2 7.1 %collective-permute-start.26 = (f32[160,512]{1,0:T(8,128)S(1)}, f32[160,512]{1,0:T(8,128)S(1)}, u32[]{:S(2)}, u32[]{:S(2)}) collective-permute-start(f32[160,512]{1,0:T(8,128)S(1)} %get-tuple-element.47), channel_id=1, source_target_pairs={{0,2},{1,5},{2,0},{3,7},{4,6},{5,1},{6,4},{7,3},{8,10},{9,13},{10,... | collective-permute-start | bytes 983048 | tf_op jit(solution)/shard_map/ppermute | solution.py:73
  173.8 9.5 %collective-permute-start.27 = (f32[160,512]{1,0:T(8,128)S(1)}, f32[160,512]{1,0:T(8,128)S(1)}, u32[]{:S(2)}, u32[]{:S(2)}) collective-permute-start(f32[160,512]{1,0:T(8,128)S(1)} %get-tuple-element.48), channel_id=1, source_target_pairs={{0,3},{1,4},{2,1},{3,6},{4,7},{5,0},{6,5},{7,2},{8,11},{9,12},{10,... | collective-permute-start | bytes 983048 | tf_op jit(solution)/shard_map/ppermute | solution.py:73
  (18 other events, 167.6 us)

commit v3 on v2

--- a/solution.py
+++ b/solution.py
@@ -118,16 +118,15 @@
     outs = refs[-4:]
     prior = refs[6 * blocks : 6 * blocks + 4]
     rows = outs[0].shape[0]
+    total = None
+    for n in range(blocks):
+        own, from_core, near_low, near_high, from_diag, x_ref = refs[6 * n : 6 * n + 6]
+        pieces = [own[...], from_core[0], near_low[0], near_high[0], from_diag[0]]
+        part = jnp.dot(jnp.concatenate(pieces, axis=0), x_ref[...], preferred_element_type=jnp.float32)
+        total = part if total is None else total + part
     for q in range(4):
-        for first in (0, rows // 2) if q == 2 else (0,):
-            total = None
-            for n in range(blocks):
-                own, from_core, near_low, near_high, from_diag, x_ref = refs[6 * n : 6 * n + 6]
-                piece = (own[...], from_core[0], near_high[0] if first else near_low[0], from_diag[0])[q]
-                part = jnp.dot(piece, x_ref[...], preferred_element_type=jnp.float32)
-                total = part if total is None else total + part
-            place = pl.ds(first, total.shape[0])
-            outs[q][place, :] = total + prior[q][place, :] if has_prior else total
+        part = total[q * rows : (q + 1) * rows, :]
+        outs[q][...] = part + prior[q][...] if has_prior else part
 
 
 def cross_add(prior, targets, received, blocks, after=()):
@@ -178,25 +177,28 @@
     count = len(tiles)
     for p in range(count):
         low = p * SUB
+        inside = (lane >= low) & (lane < low + SUB)
         rows = tiles[p]
         cols = [wide(rows[:, low + k : low + k + 1]) for k in range(SUB)]
-        inside = (lane >= low) & (lane < low + SUB)
+        below = [[wide(tiles[i][:, low + k : low + k + 1]) for k in range(SUB)] for i in range(p + 1, count)]
         rows = jnp.where(inside, jnp.where(lane - low == sub, 1.0, 0.0), rows)
+        for i in range(p + 1, count):
+            tiles[i] = jnp.where(inside, 0.0, tiles[i])
         for k in range(SUB):
             root = inverse_root(wide(cols[k][k : k + 1, :]))
             scaled = cols[k] * root
+            factors = {j: wide(scaled[j : j + 1, :]) for j in range(k + 1, SUB)}
             for j in range(k + 1, SUB):
-                cols[j] = cols[j] - scaled * wide(scaled[j : j + 1, :])
+                cols[j] = cols[j] - scaled * factors[j]
             pivot_row = wide(rows[k : k + 1, :]) * root
             rows = jnp.where(sub == k, pivot_row, jnp.where(sub > k, rows - scaled * pivot_row, rows))
+            for i in range(p + 1, count):
+                mine = below[i - p - 1]
+                scaled_below = mine[k] * root
+                for j in range(k + 1, SUB):
+                    mine[j] = mine[j] - scaled_below * factors[j]
+                tiles[i] = tiles[i] - scaled_below * pivot_row
         tiles[p] = rows
-        if p + 1 < count:
-            right = jnp.where(lane >= low + SUB, rows, 0.0)
-            change = lax.dot_general(
-                right, rows, (((0,), (0,)), ((), ())), precision=HI, preferred_element_type=jnp.float32
-            )
-            for i in range(p + 1, count):
-                tiles[i] = jnp.where(inside, 0.0, tiles[i]) - change[i * SUB : (i + 1) * SUB, :]
     return jnp.concatenate(tiles, axis=0)
 
 
@@ -399,56 +401,52 @@
     keep, give = live_halves(core, cell_counts, embeddings)
     got = send(give, CORE)
     block = join_features(core, keep, got)
-    rows = targets_by_gene.shape[0]
     line1 = send(block, LINE[0])
+    middle_own = send(block, MIDDLE)
     far_own = send(block, FAR)
 
     gram_give = gram_rows(ints(1 - c), block)
     gram_got = send(gram_give, CORE)
     gram_keep = gram_rows(ints(c), block, after=(gram_give,))
-    place = donor % 4
-    order = ints(place, place ^ 1, place ^ 2, place ^ 3)
-    mine, *others = add_split(order, [gram_keep, gram_got])
-    parts = [mine] + [send(other, PLANE[s]) for s, other in enumerate(others)]
-    plane_sum = add_all(parts, after=(far_own,))
-    near_low = pick_blocks(targets_by_gene, blocks_for(c, 1 - near_bit), half, (plane_sum,), 0, rows // 2)
-    near_low = send(near_low, NEAR)
-
+    mine, give = add_split(ints(near_bit, 1 - near_bit), [gram_keep, gram_got])
+    for_core = pick_blocks(targets_by_gene, blocks_for(1 - c, far_bit), half, after=(mine,))
+    from_core = send(for_core, CORE)
+    mine, give = add_split(ints(far_bit, 1 - far_bit), [mine, send(give, NEAR)], after=(for_core,))
+    got = send(give, FAR)
+    place = near_bit * 2 + far_bit
+    order = ints(place, place ^ jnp.where(c == 0, 2, 1), place ^ jnp.where(c == 0, 1, 2), place ^ 3)
+
+    rows = targets_by_gene.shape[0]
+    cut = 6 * rows // 10 // 16 * 16
+    near_blocks = blocks_for(c, 1 - near_bit)
+    for_near = pick_blocks(targets_by_gene, near_blocks, half, (got, far_own, line1, middle_own), 0, cut)
+    near_low = send(for_near, NEAR)
+    plane_sum = add_all([mine, got], after=(line1, middle_own))
     line_parts = [plane_sum] + [send(plane_sum, LINE[s]) for s in range(3)]
-    total = add_all(line_parts, after=(line1,))
+    total = add_all(line_parts)
 
     quarters = [total] + [send(total, PLANE[s]) for s in range(3)]
-    (late,) = copy_rows(block, ((0, half),), (total,))
-    middle_own = send(late, MIDDLE)
-    quarter = place_parts(order, quarters, (late,))
-    (late,) = copy_rows(line1, ((0, half),), (quarter,))
-    middle_outer = send(late, MIDDLE)
-    near_high = pick_blocks(
-        targets_by_gene, blocks_for(c, 1 - near_bit), half, (late,), rows // 2, rows // 2
-    )
-    gram = place_parts(ints(c, 1 - c), [quarter, send(quarter, CORE)], after=(near_high, near_low))
-    near_high = send(near_high, NEAR)
+    for_near = pick_blocks(targets_by_gene, near_blocks, half, (total,), cut, rows - cut)
+    near_high = send(for_near, NEAR)
+    quarter = place_parts(order, quarters, (for_near, near_low, from_core))
+    outward_own = send(middle_own, OUTWARD)
+    middle_outer = send(line1, MIDDLE)
+    for_diag = pick_blocks(targets_by_gene, blocks_for(1 - c, 1 - far_bit), half, (quarter,))
+    from_diag = send(for_diag, DIAG_OUT)
+    gram = place_parts(ints(c, 1 - c), [quarter, send(quarter, CORE)], after=(for_diag,))
+
     value = factor_step(0, gram)
-    for_diag = pick_blocks(targets_by_gene, blocks_for(1 - c, 1 - far_bit), half, (value,))
-    from_diag = send(for_diag, DIAG_OUT)
-    for_core = pick_blocks(targets_by_gene, blocks_for(1 - c, far_bit), half, after=(for_diag,))
-    from_core = send(for_core, CORE)
-
-    value = factor_step(1, value, after=(for_core,))
-    (late,) = copy_rows(middle_own, ((0, half),), (value, near_high))
-    outward_own = send(late, OUTWARD)
+    value = factor_step(1, value)
+    (late,) = copy_rows(middle_outer, ((0, half),), (value, near_high, outward_own))
+    outward_outer = send(late, OUTWARD)
     (late,) = copy_rows(line1, ((0, half),), (late,))
     far1 = send(late, FAR)
-    value = factor_step(2, value, after=(late,))
-    value = factor_step(3, value)
-    inverse = gram_inverse(value, math.sqrt(slots * donors))
-    (late,) = copy_rows(middle_outer, ((0, half),), (inverse,))
-    outward_outer = send(late, OUTWARD)
     is_middle = jnp.where((z == 1) | (z == 2), 1, 0)
     second = choose(ints(is_middle), outward_own, middle_own, (late,))
     far2 = send(second, FAR)
-    third = choose(ints(is_middle), outward_outer, middle_outer)
-    far3 = send(third, FAR)
+    value = factor_step(2, value, after=(second,))
+    value = factor_step(3, value)
+    inverse = gram_inverse(value, math.sqrt(slots * donors))
     second_z = jnp.where(is_middle == 1, z ^ 3, z ^ 2)
     third_z = jnp.where(is_middle == 1, z ^ 2, z ^ 3)
 
@@ -458,16 +456,15 @@
         return piece, column, k, part
 
     received = (from_core, near_low, near_high, from_diag)
-    acc = None
-    for blocks in (
-        [(block, z, far_bit), (far_own, z, 1 - far_bit), (line1, z ^ 1, far_bit)],
-        [(second, second_z, far_bit), (far1, z ^ 1, 1 - far_bit)],
-        [(third, third_z, far_bit), (far2, second_z, 1 - far_bit)],
-        [(far3, third_z, 1 - far_bit)],
-    ):
-        acc = cross_add(
-            acc, targets_by_gene, received, [cells_of(*block) for block in blocks], (inverse,) if acc is None else ()
-        )
+    def add(acc, blocks, after=()):
+        return cross_add(acc, targets_by_gene, received, [cells_of(*block) for block in blocks], after)
+
+    acc = add(None, [(block, z, far_bit), (far_own, z, 1 - far_bit), (line1, z ^ 1, far_bit)], (inverse,))
+    acc = add(acc, [(second, second_z, far_bit), (far1, z ^ 1, 1 - far_bit)])
+    third = choose(ints(is_middle), outward_outer, middle_outer, (inverse,))
+    far3 = send(third, FAR)
+    acc = add(acc, [(third, third_z, far_bit), (far2, second_z, 1 - far_bit)])
+    acc = add(acc, [(far3, third_z, 1 - far_bit)])
     own, for_other, to_near, to_diag = acc
     scaled = apply_inverse(
         inverse, [own, send(for_other, CORE), send(to_near, NEAR), send(to_diag, DIAG_BACK)]

time: 206 us -> 182 us (0.88)
  Pallas kernels: 88.3 us -> 68.8 us
  waiting for transfers between devices: 56.9 us -> 46.1 us
  blocking collectives: 19.9 us -> 22.8 us
  starting transfers between devices: 32.8 us -> 35.3 us
    pallas_call x22 -> x20, Pallas kernels: 58.2 us -> 40.5 us  [small_kernel(): pl.pallas_call(kernel, out_shape=out_shape, in_specs=[SCALARS] * len(scal...]
    ppermute x28 -> x27, waiting for transfers between devices: 56.9 us -> 46.1 us  [send(): return lax.ppermute(value, AXES, perm)]
    all_to_all x1, blocking collectives: 19.9 us -> 22.8 us  [shards(): lax.all_to_all(scaled, 'donor', split_axis=0, concat_axis=1, tiled=True)]
    ppermute x28 -> x27, starting transfers between devices: 32.8 us -> 35.3 us  [send(): return lax.ppermute(value, AXES, perm)]
    unnamed x28 -> x18, local copies, waits for them, and re-layouts: 4.84 us -> 5.16 us
  transfers between devices with their start and end apart: 28 -> 27, of which waited for: 13 -> 11; matrix products, arithmetic and copies ran while one was open for 0% -> 0% of each run, Pallas kernels for 41% -> 35%
where the time goes in v3:
time: 182 us; the launch traced here: 181 us
  Pallas kernels  68.8 us (38%)
  waiting for transfers between devices  46.1 us (25%)
  starting transfers between devices  35.3 us (19%)
  blocking collectives  22.8 us (13%)
  local copies, waits for them, and re-layouts  6.54 us (4%)
    ppermute x27, waiting for transfers between devices, send(): return lax.ppermute(value, AXES, perm)  46.1 us
    pallas_call x20, Pallas kernels, small_kernel(): pl.pallas_call(kernel, out_shape=out_shape, in_specs=[SCALARS] * len(scal...  40.5 us
    ppermute x27, starting transfers between devices, send(): return lax.ppermute(value, AXES, perm)  35.3 us
    all_to_all x1, blocking collectives, shards(): lax.all_to_all(scaled, 'donor', split_axis=0, concat_axis=1, tiled=True)  22.8 us
    pallas_call x4, Pallas kernels, cross_add(): pl.pallas_call(functools.partial(cross_kernel, prior is not None, len(blo...  16.5 us
    pallas_call x4, Pallas kernels, pick_blocks(): pl.pallas_call(functools.partial(pick_kernel, first_row), out_shape=jax.S...  11.9 us
    unnamed x18, local copies, waits for them, and re-layouts  5.16 us
  transfers between devices with their start and end apart: 27, of which 11 were waited for; matrix products, arithmetic and copies ran while one was open for 0% of the time, Pallas kernels for 35%

profile of v3, /device:TPU:0, one launch (start us, length us, event | category | flops | bytes accessed | tf_op | source)
XLA Modules:
  0.0 181.2 jit_solution(17106679947925033369)
XLA Ops:
  5.7 2.8 %collective-permute-start.4 = (bf16[1024,512]{1,0:T(8,128)(2,1)S(1)}, bf16[1024,512]{1,0:T(8,128)(2,1)}, u32[]{:S(2)}, u32[]{:S(2)}) collective-permute-start(bf16[1024,512]{1,0:T(8,128)(2,1)S(1)} %join_features.1.refs_1_.refs_5_), channel_id=1, source_target_pairs={{0,8},{1,9},{2,10},{3,11},{4,12},{5,13},{6,14},{7,15},{8,0},{9,1},... | collective-permute-start | bytes 3145736 | tf_op jit(solution)/shard_map/ppermute | solution.py:73
  12.3 3.2 %pick_blocks.4.refs_3_ = bf16[8,160,1024]{2,1,0:T(8,128)(2,1)} custom-call(s32[8]{0:T(128)S(1)} %fusion.9.index_ref, bf16[160,32768]{1,0:T(8,128)(2,1)} %refs_0_.7, f32[128,512]{1,0:T(8,128)S(1)} %get-tuple-element.29.rest_0_.refs_1_), custom_call_target="tpu_custom_call" | custom-call | flops 1 | bytes 1 | tf_op jit(solution)/shard_map/pick_blocks/pallas_call | solution.py:100
  17.2 7.7 %collective-permute-done.2.refs_2_ = f32[128,512]{1,0:T(8,128)S(1)} collective-permute-done((f32[128,512]{1,0:T(8,128)S(1)}, f32[128,512]{1,0:T(8,128)S(1)}, u32[]{:S(2)}, u32[]{:S(2)}) %collective-permute-start.2) | collective-permute-done | bytes 262176 | tf_op jit(solution)/shard_map/ppermute | solution.py:73
  26.8 3.8 %collective-permute-done.3.refs_1_.rest_0_ = f32[64,512]{1,0:T(8,128)S(1)} collective-permute-done((f32[64,512]{1,0:T(8,128)S(1)}, f32[64,512]{1,0:T(8,128)S(1)}, u32[]{:S(2)}, u32[]{:S(2)}) %collective-permute-start.3) | collective-permute-done | bytes 131104 | tf_op jit(solution)/shard_map/ppermute | solution.py:73
  32.3 2.9 %pick_blocks.6 = bf16[8,96,1024]{2,1,0:T(8,128)(2,1)} custom-call(s32[8]{0:T(128)S(1)} %fusion.7.index_ref, bf16[160,32768]{1,0:T(8,128)(2,1)} %refs_0_.7, f32[64,512]{1,0:T(8,128)S(1)} %collective-permute-done.3.refs_1_.rest_0_, bf16[1024,512]{1,0:T(8,128)(2,1)S(1)} %collective-permute-done.12.rest_1_.refs_11_, ...), custom_call_target="tpu_custom_call" | custom-call | flops 1 | bytes 1 | tf_op jit(solution)/shard_map/pick_blocks/pallas_call | solution.py:100
  37.9 4.7 %collective-permute-start.6 = (f32[64,512]{1,0:T(8,128)S(1)}, f32[64,512]{1,0:T(8,128)S(1)}, u32[]{:S(2)}, u32[]{:S(2)}) collective-permute-start(f32[64,512]{1,0:T(8,128)S(1)} %add_all.2.refs_0_), channel_id=1, source_target_pairs={{0,8},{1,9},{2,10},{3,11},{4,12},{5,13},{6,14},{7,15},{8,0},{9,1},... | collective-permute-start | bytes 393224 | tf_op jit(solution)/shard_map/ppermute | solution.py:73
  46.7 8.1 %collective-permute-done.7.refs_2_ = f32[64,512]{1,0:T(8,128)S(1)} collective-permute-done((f32[64,512]{1,0:T(8,128)S(1)}, f32[64,512]{1,0:T(8,128)S(1)}, u32[]{:S(2)}, u32[]{:S(2)}) %collective-permute-start.7) | collective-permute-done | bytes 131104 | tf_op jit(solution)/shard_map/ppermute | solution.py:73
  58.4 2.6 %pick_blocks.5.refs_5_ = bf16[8,64,1024]{2,1,0:T(8,128)(2,1)} custom-call(s32[8]{0:T(128)S(1)} %fusion.7.index_ref, bf16[160,32768]{1,0:T(8,128)(2,1)} %refs_0_.7, f32[64,512]{1,0:T(8,128)S(1)} %add_all.3.rest_0_.refs_1_), custom_call_target="tpu_custom_call" | custom-call | flops 1 | bytes 1 | tf_op jit(solution)/shard_map/pick_blocks/pallas_call | solution.py:100
  66.6 3.2 %pick_blocks.7.refs_3_ = bf16[8,160,1024]{2,1,0:T(8,128)(2,1)} custom-call(s32[8]{0:T(128)S(1)} %fusion.8.index_ref, bf16[160,32768]{1,0:T(8,128)(2,1)} %refs_0_.7, f32[256,512]{1,0:T(8,128)S(1)} %place_parts.2.rest_0_.refs_1_), custom_call_target="tpu_custom_call" | custom-call | flops 1 | bytes 1 | tf_op jit(solution)/shard_map/pick_blocks/pallas_call | solution.py:100
  72.9 6.3 %factor_step.4.refs_0_ = f32[512,512]{1,0:T(8,128)S(1)} custom-call(f32[512,512]{1,0:T(8,128)S(1)} %place_parts.3.refs_0_), custom_call_target="tpu_custom_call" | custom-call | flops 1 | bytes 1 | tf_op jit(solution)/shard_map/factor_step/pallas_call | solution.py:232
  79.2 6.1 %factor_step.5.refs_1_.refs_0_ = f32[512,512]{1,0:T(8,128)S(1)} custom-call(f32[512,512]{1,0:T(8,128)S(1)} %factor_step.4.refs_0_), custom_call_target="tpu_custom_call" | custom-call | flops 1 | bytes 1 | tf_op jit(solution)/shard_map/factor_step/pallas_call | solution.py:232
  85.4 7.1 %collective-permute-done.16.refs_3_.refs_1_ = bf16[1024,512]{1,0:T(8,128)(2,1)} collective-permute-done((bf16[1024,512]{1,0:T(8,128)(2,1)}, bf16[1024,512]{1,0:T(8,128)(2,1)}, u32[]{:S(2)}, u32[]{:S(2)}) %collective-permute-start.16) | collective-permute-done | bytes 1048608 | tf_op jit(solution)/shard_map/ppermute | solution.py:73
  100.2 2.6 %choose.2.refs_1_.refs_5_ = bf16[1024,512]{1,0:T(8,128)(2,1)} custom-call(s32[1]{0:T(128)} %bitcast.10.refs_0_, bf16[1024,512]{1,0:T(8,128)(2,1)} %collective-permute-done.16.refs_3_.refs_1_, bf16[1024,512]{1,0:T(8,128)(2,1)} %collective-permute-done.5.refs_3_.rest_3_.refs_2_, bf16[1024,512]{1,0:T(8,128)(2,1)} %copy_rows.3.refs_3_), custom_call_target="tpu_custom_call" | custom-call | flops 1 | bytes 1 | tf_op jit(solution)/shard_map/choose/pallas_call | solution.py:232
  103.2 6.0 %factor_step.6.refs_0_ = f32[512,512]{1,0:T(8,128)S(1)} custom-call(f32[512,512]{1,0:T(8,128)S(1)} %factor_step.5.refs_1_.refs_0_, bf16[1024,512]{1,0:T(8,128)(2,1)} %choose.2.refs_1_.refs_5_), custom_call_target="tpu_custom_call" | custom-call | flops 1 | bytes 1 | tf_op jit(solution)/shard_map/factor_step/pallas_call | solution.py:232
  109.2 5.6 %factor_step.7.refs_0_ = f32[512,512]{1,0:T(8,128)S(1)} custom-call(f32[512,512]{1,0:T(8,128)S(1)} %factor_step.6.refs_0_), custom_call_target="tpu_custom_call" | custom-call | flops 1 | bytes 1 | tf_op jit(solution)/shard_map/factor_step/pallas_call | solution.py:232
  116.6 4.7 %collective-permute-done.20.refs_1_ = bf16[1024,512]{1,0:T(8,128)(2,1)} collective-permute-done((bf16[1024,512]{1,0:T(8,128)(2,1)}, bf16[1024,512]{1,0:T(8,128)(2,1)}, u32[]{:S(2)}, u32[]{:S(2)}) %collective-permute-start.20) | collective-permute-done | bytes 1048608 | tf_op jit(solution)/shard_map/ppermute | solution.py:73
  124.9 2.6 %collective-permute-start.21 = (bf16[1024,512]{1,0:T(8,128)(2,1)}, bf16[1024,512]{1,0:T(8,128)(2,1)}, u32[]{:S(2)}, u32[]{:S(2)}) collective-permute-start(bf16[1024,512]{1,0:T(8,128)(2,1)} %choose.3.refs_5_), channel_id=1, source_target_pairs={{0,4},{1,3},{2,6},{3,1},{4,0},{5,7},{6,2},{7,5},{8,12},{9,11},{10,... | collective-permute-start | bytes 3145736 | tf_op jit(solution)/shard_map/ppermute | solution.py:73
  129.2 5.0 %cross_add.4 = (f32[160,512]{1,0:T(8,128)S(1)}, f32[160,512]{1,0:T(8,128)S(1)}, f32[160,512]{1,0:T(8,128)S(1)}, f32[160,512]{1,0:T(8,128)S(1)}) custom-call(s32[6]{0:T(128)S(1)} %stack.143.index_ref, bf16[160,32768]{1,0:T(8,128)(2,1)} %refs_0_.7, bf16[8,160,1024]{2,1,0:T(8,128)(2,1)} %collective-permute-done.14.refs_7_.refs_1_.refs_13_, ...), custom_call_target="tpu_custom_call" | custom-call | flops 1 | bytes 1 | tf_op jit(solution)/shard_map/cross_add/pallas_call | solution.py:148
  134.3 4.2 %cross_add.5 = (f32[160,512]{1,0:T(8,128)S(1)}, f32[160,512]{1,0:T(8,128)S(1)}, f32[160,512]{1,0:T(8,128)S(1)}, f32[160,512]{1,0:T(8,128)S(1)}) custom-call(s32[4]{0:T(128)S(1)} %pad_add_fusion.6.index_ref, bf16[160,32768]{1,0:T(8,128)(2,1)} %refs_0_.7, ...), custom_call_target="tpu_custom_call", output_to_operand_aliasing={{0}: (13, {}), {1}: (14, {}), {2}: (15, {}), {3}: (16, {})} | custom-call | flops 1 | bytes 1 | tf_op jit(solution)/shard_map/cross_add/pallas_call | solution.py:148
  138.5 4.3 %cross_add.6 = (f32[160,512]{1,0:T(8,128)S(1)}, f32[160,512]{1,0:T(8,128)S(1)}, f32[160,512]{1,0:T(8,128)S(1)}, f32[160,512]{1,0:T(8,128)S(1)}) custom-call(s32[4]{0:T(128)S(1)} %pad_add_fusion.5.index_ref, bf16[160,32768]{1,0:T(8,128)(2,1)} %refs_0_.7, ...), custom_call_target="tpu_custom_call", output_to_operand_aliasing={{0}: (13, {}), {1}: (14, {}), {2}: (15, {}), {3}: (16, {})} | custom-call | flops 1 | bytes 1 | tf_op jit(solution)/shard_map/cross_add/pallas_call | solution.py:148
  142.8 2.9 %cross_add.7 = (f32[160,512]{1,0:T(8,128)S(1)}, f32[160,512]{1,0:T(8,128)S(1)}, f32[160,512]{1,0:T(8,128)S(1)}, f32[160,512]{1,0:T(8,128)S(1)}) custom-call(s32[2]{0:T(128)S(1)} %pad_add_fusion.4.index_ref, bf16[160,32768]{1,0:T(8,128)(2,1)} %refs_0_.7, ...), custom_call_target="tpu_custom_call", output_to_operand_aliasing={{0}: (7, {}), {1}: (8, {}), {2}: (9, {}), {3}: (10, {})} | custom-call | flops 1 | bytes 1 | tf_op jit(solution)/shard_map/cross_add/pallas_call | solution.py:148
  147.5 5.5 %collective-permute-done.25.refs_3_ = f32[160,512]{1,0:T(8,128)S(1)} collective-permute-done((f32[160,512]{1,0:T(8,128)S(1)}, f32[160,512]{1,0:T(8,128)S(1)}, u32[]{:S(2)}, u32[]{:S(2)}) %collective-permute-start.25) | collective-permute-done | bytes 327712 | tf_op jit(solution)/shard_map/ppermute | solution.py:73
  153.0 3.0 %collective-permute-done.26.refs_4_ = f32[160,512]{1,0:T(8,128)S(1)} collective-permute-done((f32[160,512]{1,0:T(8,128)S(1)}, f32[160,512]{1,0:T(8,128)S(1)}, u32[]{:S(2)}, u32[]{:S(2)}) %collective-permute-start.26) | collective-permute-done | bytes 327712 | tf_op jit(solution)/shard_map/ppermute | solution.py:73
  157.1 22.8 %all_to_all.19 = f32[16,32,160]{2,1,0:T(8,128)S(1)} all-to-all(f32[16,32,160]{2,1,0:T(8,128)S(1)} %bitcast.29), channel_id=1, replica_groups=mesh['donor'=16,'gene'=2] {'donor'}, dimensions={0} | all-to-all | bytes 655360 | tf_op jit(solution)/shard_map/all_to_all | solution.py:472
  (90 shorter events, 52.4 us)
Async XLA Ops:
  4.8 7.0 %collective-permute-start.1 = (f32[256,512]{1,0:T(8,128)S(1)}, f32[256,512]{1,0:T(8,128)S(1)}, u32[]{:S(2)}, u32[]{:S(2)}) collective-permute-start(f32[256,512]{1,0:T(8,128)S(1)} %gram_rows.2.refs_2_), channel_id=1, source_target_pairs={{0,1},{1,0},{2,3},{3,2},{4,5},{5,4},{6,7},{7,6},{8,9},{9,8},{10,11... | collective-permute-start | bytes 1572872 | tf_op jit(solution)/shard_map/ppermute | solution.py:73
  5.7 26.6 %collective-permute-start.4 = (bf16[1024,512]{1,0:T(8,128)(2,1)S(1)}, bf16[1024,512]{1,0:T(8,128)(2,1)}, u32[]{:S(2)}, u32[]{:S(2)}) collective-permute-start(bf16[1024,512]{1,0:T(8,128)(2,1)S(1)} %join_features.1.refs_1_.refs_5_), channel_id=1, source_target_pairs={{0,8},{1,9},{2,10},{3,11},{4,12},{5,13},{6,14},{7,15},{8,0},{9,1},... | collective-permute-start | bytes 3145736 | tf_op jit(solution)/shard_map/ppermute | solution.py:73
  8.5 23.8 %collective-permute-start.5 = (bf16[1024,512]{1,0:T(8,128)(2,1)S(1)}, bf16[1024,512]{1,0:T(8,128)(2,1)}, u32[]{:S(2)}, u32[]{:S(2)}) collective-permute-start(bf16[1024,512]{1,0:T(8,128)(2,1)S(1)} %join_features.1.refs_1_.refs_5_), channel_id=1, source_target_pairs={{8,16},{9,17},{10,18},{11,19},{12,20},{13,21},{14,22},{15,23},{16,... | collective-permute-start | bytes 3145736 | tf_op jit(solution)/shard_map/ppermute | solution.py:73
  10.2 22.2 %collective-permute-start.12 = (bf16[1024,512]{1,0:T(8,128)(2,1)S(1)}, bf16[1024,512]{1,0:T(8,128)(2,1)S(1)}, u32[]{:S(2)}, u32[]{:S(2)}) collective-permute-start(bf16[1024,512]{1,0:T(8,128)(2,1)S(1)} %join_features.1.refs_1_.refs_5_), channel_id=1, source_target_pairs={{0,4},{1,3},{2,6},{3,1},{4,0},{5,7},{6,2},{7,5},{8,12},{9,11},{10,... | collective-permute-start | bytes 3145736 | tf_op jit(solution)/shard_map/ppermute | solution.py:73
  15.5 49.9 %collective-permute-start.14 = (bf16[8,160,1024]{2,1,0:T(8,128)(2,1)}, bf16[8,160,1024]{2,1,0:T(8,128)(2,1)}, u32[]{:S(2)}, u32[]{:S(2)}) collective-permute-start(bf16[8,160,1024]{2,1,0:T(8,128)(2,1)} %pick_blocks.4.refs_3_), channel_id=1, source_target_pairs={{0,1},{1,0},{2,3},{3,2},{4,5},{5,4},{6,7},{7,6},{8,9},{9,8},{10,11... | collective-permute-start | bytes 7864328 | tf_op jit(solution)/shard_map/ppermute | solution.py:73
  15.6 9.3 %collective-permute-start.2 = (f32[128,512]{1,0:T(8,128)S(1)}, f32[128,512]{1,0:T(8,128)S(1)}, u32[]{:S(2)}, u32[]{:S(2)}) collective-permute-start(f32[128,512]{1,0:T(8,128)S(1)} %get-tuple-element.30), channel_id=1, source_target_pairs={{0,2},{1,5},{2,0},{3,7},{4,6},{5,1},{6,4},{7,3},{8,10},{9,13},{10,... | collective-permute-start | bytes 786440 | tf_op jit(solution)/shard_map/ppermute | solution.py:73
  25.5 5.0 %collective-permute-start.3 = (f32[64,512]{1,0:T(8,128)S(1)}, f32[64,512]{1,0:T(8,128)S(1)}, u32[]{:S(2)}, u32[]{:S(2)}) collective-permute-start(f32[64,512]{1,0:T(8,128)S(1)} %get-tuple-element.32), channel_id=1, source_target_pairs={{0,4},{1,3},{2,6},{3,1},{4,0},{5,7},{6,2},{7,5},{8,12},{9,11},{10,... | collective-permute-start | bytes 393224 | tf_op jit(solution)/shard_map/ppermute | solution.py:73
  36.2 29.2 %collective-permute-start.13 = (bf16[8,96,1024]{2,1,0:T(8,128)(2,1)}, bf16[8,96,1024]{2,1,0:T(8,128)(2,1)S(1)}, u32[]{:S(2)}, u32[]{:S(2)}) collective-permute-start(bf16[8,96,1024]{2,1,0:T(8,128)(2,1)} %pick_blocks.6), channel_id=1, source_target_pairs={{0,2},{1,5},{2,0},{3,7},{4,6},{5,1},{6,4},{7,3},{8,10},{9,13},{10,... | collective-permute-start | bytes 4718600 | tf_op jit(solution)/shard_map/ppermute | solution.py:73
  37.9 8.8 %collective-permute-start.6 = (f32[64,512]{1,0:T(8,128)S(1)}, f32[64,512]{1,0:T(8,128)S(1)}, u32[]{:S(2)}, u32[]{:S(2)}) collective-permute-start(f32[64,512]{1,0:T(8,128)S(1)} %add_all.2.refs_0_), channel_id=1, source_target_pairs={{0,8},{1,9},{2,10},{3,11},{4,12},{5,13},{6,14},{7,15},{8,0},{9,1},... | collective-permute-start | bytes 393224 | tf_op jit(solution)/shard_map/ppermute | solution.py:73
  42.6 12.2 %collective-permute-start.7 = (f32[64,512]{1,0:T(8,128)S(1)}, f32[64,512]{1,0:T(8,128)S(1)}, u32[]{:S(2)}, u32[]{:S(2)}) collective-permute-start(f32[64,512]{1,0:T(8,128)S(1)} %add_all.2.refs_0_), channel_id=1, source_target_pairs={{0,16},{1,17},{2,18},{3,19},{4,20},{5,21},{6,22},{7,23},{8,24},{9,... | collective-permute-start | bytes 393224 | tf_op jit(solution)/shard_map/ppermute | solution.py:73
  43.8 11.0 %collective-permute-start.8 = (f32[64,512]{1,0:T(8,128)S(1)}, f32[64,512]{1,0:T(8,128)S(1)}, u32[]{:S(2)}, u32[]{:S(2)}) collective-permute-start(f32[64,512]{1,0:T(8,128)S(1)} %add_all.2.refs_0_), channel_id=1, source_target_pairs={{0,24},{1,25},{2,26},{3,27},{4,28},{5,29},{6,30},{7,31},{8,16},{9,... | collective-permute-start | bytes 393224 | tf_op jit(solution)/shard_map/ppermute | solution.py:73
  54.8 6.2 %collective-permute-start.10 = (f32[64,512]{1,0:T(8,128)S(1)}, f32[64,512]{1,0:T(8,128)S(1)}, u32[]{:S(2)}, u32[]{:S(2)}) collective-permute-start(f32[64,512]{1,0:T(8,128)S(1)} %add_all.3.rest_0_.refs_1_), channel_id=1, source_target_pairs={{0,4},{1,5},{2,6},{3,7},{4,0},{5,1},{6,2},{7,3},{8,12},{9,13},{10,... | collective-permute-start | bytes 393224 | tf_op jit(solution)/shard_map/ppermute | solution.py:73
  55.4 7.3 %collective-permute-start.11 = (f32[64,512]{1,0:T(8,128)S(1)}, f32[64,512]{1,0:T(8,128)S(1)}, u32[]{:S(2)}, u32[]{:S(2)}) collective-permute-start(f32[64,512]{1,0:T(8,128)S(1)} %add_all.3.rest_0_.refs_1_), channel_id=1, source_target_pairs={{0,6},{1,7},{2,4},{3,5},{4,2},{5,3},{6,0},{7,1},{8,14},{9,15},{10,... | collective-permute-start | bytes 393224 | tf_op jit(solution)/shard_map/ppermute | solution.py:73
  57.6 6.4 %collective-permute-start.9 = (f32[64,512]{1,0:T(8,128)S(1)}, f32[64,512]{1,0:T(8,128)S(1)}, u32[]{:S(2)}, u32[]{:S(2)}) collective-permute-start(f32[64,512]{1,0:T(8,128)S(1)} %add_all.3.rest_0_.refs_1_), channel_id=1, source_target_pairs={{0,2},{1,3},{2,0},{3,1},{4,6},{5,7},{6,4},{7,5},{8,10},{9,11},{10,... | collective-permute-start | bytes 393224 | tf_op jit(solution)/shard_map/ppermute | solution.py:73
  61.0 24.4 %collective-permute-start.17 = (bf16[1024,512]{1,0:T(8,128)(2,1)}, bf16[1024,512]{1,0:T(8,128)(2,1)}, u32[]{:S(2)}, u32[]{:S(2)}) collective-permute-start(bf16[1024,512]{1,0:T(8,128)(2,1)} %collective-permute-done.4.refs_2_.rest_2_.refs_0_.refs_17_), channel_id=1, source_target_pairs={{8,16},{9,17},{10,18},{11,19},{12,20},{13,21},{14,22},{15,23},{16,... | collective-permute-start | bytes 3145736 | tf_op jit(solution)/shard_map/ppermute | solution.py:73
  62.7 29.8 %collective-permute-start.16 = (bf16[1024,512]{1,0:T(8,128)(2,1)}, bf16[1024,512]{1,0:T(8,128)(2,1)}, u32[]{:S(2)}, u32[]{:S(2)}) collective-permute-start(bf16[1024,512]{1,0:T(8,128)(2,1)} %collective-permute-done.5.refs_3_.rest_3_.refs_2_), channel_id=1, source_target_pairs={{8,0},{9,1},{10,2},{11,3},{12,4},{13,5},{14,6},{15,7},{16,24},{17,... | collective-permute-start | bytes 3145736 | tf_op jit(solution)/shard_map/ppermute | solution.py:73
  64.0 28.5 %collective-permute-start.18 = (bf16[8,64,1024]{2,1,0:T(8,128)(2,1)}, bf16[8,64,1024]{2,1,0:T(8,128)(2,1)S(1)}, u32[]{:S(2)}, u32[]{:S(2)}) collective-permute-start(bf16[8,64,1024]{2,1,0:T(8,128)(2,1)} %pick_blocks.5.refs_5_), channel_id=1, source_target_pairs={{0,2},{1,5},{2,0},{3,7},{4,6},{5,1},{6,4},{7,3},{8,10},{9,13},{10,... | collective-permute-start | bytes 3145736 | tf_op jit(solution)/shard_map/ppermute | solution.py:73
  69.8 58.1 %collective-permute-start.19 = (bf16[8,160,1024]{2,1,0:T(8,128)(2,1)}, bf16[8,160,1024]{2,1,0:T(8,128)(2,1)}, u32[]{:S(2)}, u32[]{:S(2)}) collective-permute-start(bf16[8,160,1024]{2,1,0:T(8,128)(2,1)} %pick_blocks.7.refs_3_), channel_id=1, source_target_pairs={{0,5},{1,2},{2,7},{3,0},{4,1},{5,6},{6,3},{7,4},{8,13},{9,10},{10,... | collective-permute-start | bytes 7864328 | tf_op jit(solution)/shard_map/ppermute | solution.py:73
  94.7 26.5 %collective-permute-start.20 = (bf16[1024,512]{1,0:T(8,128)(2,1)}, bf16[1024,512]{1,0:T(8,128)(2,1)}, u32[]{:S(2)}, u32[]{:S(2)}) collective-permute-start(bf16[1024,512]{1,0:T(8,128)(2,1)} %copy_rows.2.refs_1_), channel_id=1, source_target_pairs={{8,0},{9,1},{10,2},{11,3},{12,4},{13,5},{14,6},{15,7},{16,24},{17,... | collective-permute-start | bytes 3145736 | tf_op jit(solution)/shard_map/ppermute | solution.py:73
  98.5 35.7 %collective-permute-start.23 = (bf16[1024,512]{1,0:T(8,128)(2,1)}, bf16[1024,512]{1,0:T(8,128)(2,1)}, u32[]{:S(2)}, u32[]{:S(2)}) collective-permute-start(bf16[1024,512]{1,0:T(8,128)(2,1)} %copy_rows.3.refs_3_), channel_id=1, source_target_pairs={{0,4},{1,3},{2,6},{3,1},{4,0},{5,7},{6,2},{7,5},{8,12},{9,11},{10,... | collective-permute-start | bytes 3145736 | tf_op jit(solution)/shard_map/ppermute | solution.py:73
  102.8 35.7 %collective-permute-start.22 = (bf16[1024,512]{1,0:T(8,128)(2,1)}, bf16[1024,512]{1,0:T(8,128)(2,1)}, u32[]{:S(2)}, u32[]{:S(2)}) collective-permute-start(bf16[1024,512]{1,0:T(8,128)(2,1)} %choose.2.refs_1_.refs_5_), channel_id=1, source_target_pairs={{0,4},{1,3},{2,6},{3,1},{4,0},{5,7},{6,2},{7,5},{8,12},{9,11},{10,... | collective-permute-start | bytes 3145736 | tf_op jit(solution)/shard_map/ppermute | solution.py:73
  124.9 17.9 %collective-permute-start.21 = (bf16[1024,512]{1,0:T(8,128)(2,1)}, bf16[1024,512]{1,0:T(8,128)(2,1)}, u32[]{:S(2)}, u32[]{:S(2)}) collective-permute-start(bf16[1024,512]{1,0:T(8,128)(2,1)} %choose.3.refs_5_), channel_id=1, source_target_pairs={{0,4},{1,3},{2,6},{3,1},{4,0},{5,7},{6,2},{7,5},{8,12},{9,11},{10,... | collective-permute-start | bytes 3145736 | tf_op jit(solution)/shard_map/ppermute | solution.py:73
  145.9 7.1 %collective-permute-start.25 = (f32[160,512]{1,0:T(8,128)S(1)}, f32[160,512]{1,0:T(8,128)S(1)}, u32[]{:S(2)}, u32[]{:S(2)}) collective-permute-start(f32[160,512]{1,0:T(8,128)S(1)} %get-tuple-element.47), channel_id=1, source_target_pairs={{0,2},{1,5},{2,0},{3,7},{4,6},{5,1},{6,4},{7,3},{8,10},{9,13},{10,... | collective-permute-start | bytes 983048 | tf_op jit(solution)/shard_map/ppermute | solution.py:73
  147.4 8.6 %collective-permute-start.26 = (f32[160,512]{1,0:T(8,128)S(1)}, f32[160,512]{1,0:T(8,128)S(1)}, u32[]{:S(2)}, u32[]{:S(2)}) collective-permute-start(f32[160,512]{1,0:T(8,128)S(1)} %get-tuple-element.48), channel_id=1, source_target_pairs={{0,3},{1,4},{2,1},{3,6},{4,7},{5,0},{6,5},{7,2},{8,11},{9,12},{10,... | collective-permute-start | bytes 983048 | tf_op jit(solution)/shard_map/ppermute | solution.py:73
  (12 other events, 54.0 us)

commit v4 on v3

--- a/solution.py
+++ b/solution.py
@@ -10,7 +10,7 @@
 
 AXES = ("donor", "gene")
 HI = lax.Precision.HIGHEST
-VMEM_BYTES = 48 * 1024 * 1024
+VMEM_BYTES = 40 * 1024 * 1024
 FACTOR_BYTES = 1
 
 

time: 182 us -> 181 us (level)
  local copies, waits for them, and re-layouts: 6.54 us -> 15.7 us
  waiting for transfers between devices: 46.1 us -> 40.7 us
  starting transfers between devices: 35.3 us -> 33.2 us
    unnamed x18 -> x30, local copies, waits for them, and re-layouts: 5.16 us -> 14.3 us
    ppermute x27, waiting for transfers between devices: 46.1 us -> 40.7 us  [send(): return lax.ppermute(value, AXES, perm)]
    pallas_call x4, Pallas kernels: 11.9 us -> 9.47 us  [pick_blocks(): pl.pallas_call(functools.partial(pick_kernel, first_row), out_shape=jax.S...]
    ppermute x27, starting transfers between devices: 35.3 us -> 33.2 us  [send(): return lax.ppermute(value, AXES, perm)]
  transfers between devices with their start and end apart: 27 -> 27, of which waited for: 11 -> 12; matrix products, arithmetic and copies ran while one was open for 0% -> 0% of each run, Pallas kernels for 35% -> 35%
where the time goes in v4:
time: 181 us
  Pallas kernels  67.6 us (37%)
  waiting for transfers between devices  40.7 us (22%)
  starting transfers between devices  33.2 us (18%)
  blocking collectives  22.1 us (12%)
  local copies, waits for them, and re-layouts  15.7 us (9%)
    pallas_call x20, Pallas kernels, small_kernel(): pl.pallas_call(kernel, out_shape=out_shape, in_specs=[SCALARS] * len(scal...  41.3 us
    ppermute x27, waiting for transfers between devices, send(): return lax.ppermute(value, AXES, perm)  40.7 us
    ppermute x27, starting transfers between devices, send(): return lax.ppermute(value, AXES, perm)  33.2 us
    all_to_all x1, blocking collectives, shards(): lax.all_to_all(scaled, 'donor', split_axis=0, concat_axis=1, tiled=True)  22.1 us
    pallas_call x4, Pallas kernels, cross_add(): pl.pallas_call(functools.partial(cross_kernel, prior is not None, len(blo...  16.8 us
    unnamed x30, local copies, waits for them, and re-layouts  14.3 us
    pallas_call x4, Pallas kernels, pick_blocks(): pl.pallas_call(functools.partial(pick_kernel, first_row), out_shape=jax.S...  9.47 us
  transfers between devices with their start and end apart: 27, of which 12 were waited for; matrix products, arithmetic and copies ran while one was open for 0% of the time, Pallas kernels for 35%

profile of v4, /device:TPU:0, one launch (start us, length us, event | category | flops | bytes accessed | tf_op | source)
XLA Modules:
  0.0 180.8 jit_solution(7180312764056040266)
XLA Ops:
  5.7 2.8 %collective-permute-start.4 = (bf16[1024,512]{1,0:T(8,128)(2,1)S(1)}, bf16[1024,512]{1,0:T(8,128)(2,1)}, u32[]{:S(2)}, u32[]{:S(2)}) collective-permute-start(bf16[1024,512]{1,0:T(8,128)(2,1)S(1)} %join_features.1.refs_1_.refs_5_), channel_id=1, source_target_pairs={{0,8},{1,9},{2,10},{3,11},{4,12},{5,13},{6,14},{7,15},{8,0},{9,1},... | collective-permute-start | bytes 3145736 | tf_op jit(solution)/shard_map/ppermute | solution.py:73
  12.3 4.0 %copy-done = bf16[160,32768]{1,0:T(8,128)(2,1)S(1)} copy-done((bf16[160,32768]{1,0:T(8,128)(2,1)S(1)}, bf16[160,32768]{1,0:T(8,128)(2,1)}, u32[]{:S(2)}) %copy-start) | copy-done | bytes 10485784
  16.3 2.3 %pick_blocks.4.refs_3_ = bf16[8,160,1024]{2,1,0:T(8,128)(2,1)} custom-call(s32[8]{0:T(128)S(1)} %fusion.9.index_ref, bf16[160,32768]{1,0:T(8,128)(2,1)S(1)} %copy-done, f32[128,512]{1,0:T(8,128)S(1)} %get-tuple-element.29.rest_0_.refs_1_), custom_call_target="tpu_custom_call" | custom-call | flops 1 | bytes 1 | tf_op jit(solution)/shard_map/pick_blocks/pallas_call | solution.py:100
  20.4 6.5 %collective-permute-done.2.refs_2_ = f32[128,512]{1,0:T(8,128)S(1)} collective-permute-done((f32[128,512]{1,0:T(8,128)S(1)}, f32[128,512]{1,0:T(8,128)S(1)}, u32[]{:S(2)}, u32[]{:S(2)}) %collective-permute-start.2) | collective-permute-done | bytes 262176 | tf_op jit(solution)/shard_map/ppermute | solution.py:73
  31.3 3.6 %collective-permute-done.3.refs_1_.rest_0_ = f32[64,512]{1,0:T(8,128)S(1)} collective-permute-done((f32[64,512]{1,0:T(8,128)}, f32[64,512]{1,0:T(8,128)S(1)}, u32[]{:S(2)}, u32[]{:S(2)}) %collective-permute-start.3) | collective-permute-done | bytes 131104 | tf_op jit(solution)/shard_map/ppermute | solution.py:73
  35.0 2.9 %pick_blocks.6 = bf16[8,96,1024]{2,1,0:T(8,128)(2,1)} custom-call(s32[8]{0:T(128)S(1)} %fusion.7.index_ref, bf16[160,32768]{1,0:T(8,128)(2,1)} %refs_0_.7, f32[64,512]{1,0:T(8,128)S(1)} %collective-permute-done.3.refs_1_.rest_0_, bf16[1024,512]{1,0:T(8,128)(2,1)} %collective-permute-done.12.rest_1_.refs_11_, ...), custom_call_target="tpu_custom_call" | custom-call | flops 1 | bytes 1 | tf_op jit(solution)/shard_map/pick_blocks/pallas_call | solution.py:100
  39.5 3.3 %collective-permute-start.6 = (f32[64,512]{1,0:T(8,128)S(1)}, f32[64,512]{1,0:T(8,128)S(1)}, u32[]{:S(2)}, u32[]{:S(2)}) collective-permute-start(f32[64,512]{1,0:T(8,128)S(1)} %add_all.2.refs_0_), channel_id=1, source_target_pairs={{0,8},{1,9},{2,10},{3,11},{4,12},{5,13},{6,14},{7,15},{8,0},{9,1},... | collective-permute-start | bytes 393224 | tf_op jit(solution)/shard_map/ppermute | solution.py:73
  46.7 7.7 %collective-permute-done.7.refs_2_ = f32[64,512]{1,0:T(8,128)S(1)} collective-permute-done((f32[64,512]{1,0:T(8,128)S(1)}, f32[64,512]{1,0:T(8,128)S(1)}, u32[]{:S(2)}, u32[]{:S(2)}) %collective-permute-start.7) | collective-permute-done | bytes 131104 | tf_op jit(solution)/shard_map/ppermute | solution.py:73
  67.3 4.0 %copy-done.1 = bf16[160,32768]{1,0:T(8,128)(2,1)S(1)} copy-done((bf16[160,32768]{1,0:T(8,128)(2,1)S(1)}, bf16[160,32768]{1,0:T(8,128)(2,1)}, u32[]{:S(2)}) %copy-start.1) | copy-done | bytes 10485784
  76.7 6.3 %factor_step.4.refs_0_ = f32[512,512]{1,0:T(8,128)S(1)} custom-call(f32[512,512]{1,0:T(8,128)S(1)} %place_parts.3.refs_0_), custom_call_target="tpu_custom_call" | custom-call | flops 1 | bytes 1 | tf_op jit(solution)/shard_map/factor_step/pallas_call | solution.py:232
  83.0 6.1 %factor_step.5.refs_1_.refs_0_ = f32[512,512]{1,0:T(8,128)S(1)} custom-call(f32[512,512]{1,0:T(8,128)S(1)} %factor_step.4.refs_0_), custom_call_target="tpu_custom_call" | custom-call | flops 1 | bytes 1 | tf_op jit(solution)/shard_map/factor_step/pallas_call | solution.py:232
  89.2 3.3 %collective-permute-done.16.refs_3_.refs_1_ = bf16[1024,512]{1,0:T(8,128)(2,1)} collective-permute-done((bf16[1024,512]{1,0:T(8,128)(2,1)}, bf16[1024,512]{1,0:T(8,128)(2,1)}, u32[]{:S(2)}, u32[]{:S(2)}) %collective-permute-start.16) | collective-permute-done | bytes 1048608 | tf_op jit(solution)/shard_map/ppermute | solution.py:73
  99.8 2.8 %choose.2.refs_1_.refs_5_ = bf16[1024,512]{1,0:T(8,128)(2,1)} custom-call(s32[1]{0:T(128)} %bitcast.10.refs_0_, bf16[1024,512]{1,0:T(8,128)(2,1)} %collective-permute-done.16.refs_3_.refs_1_, bf16[1024,512]{1,0:T(8,128)(2,1)} %collective-permute-done.5.refs_3_.rest_3_.refs_2_, bf16[1024,512]{1,0:T(8,128)(2,1)} %copy_rows.3.refs_3_), custom_call_target="tpu_custom_call" | custom-call | flops 1 | bytes 1 | tf_op jit(solution)/shard_map/choose/pallas_call | solution.py:232
  103.4 6.0 %factor_step.6.refs_0_ = f32[512,512]{1,0:T(8,128)S(1)} custom-call(f32[512,512]{1,0:T(8,128)S(1)} %copy-done.8, bf16[1024,512]{1,0:T(8,128)(2,1)} %choose.2.refs_1_.refs_5_), custom_call_target="tpu_custom_call" | custom-call | flops 1 | bytes 1 | tf_op jit(solution)/shard_map/factor_step/pallas_call | solution.py:232
  109.4 5.6 %factor_step.7.refs_0_ = f32[512,512]{1,0:T(8,128)S(1)} custom-call(f32[512,512]{1,0:T(8,128)S(1)} %factor_step.6.refs_0_), custom_call_target="tpu_custom_call" | custom-call | flops 1 | bytes 1 | tf_op jit(solution)/shard_map/factor_step/pallas_call | solution.py:232
  116.8 5.3 %collective-permute-done.20.refs_1_ = bf16[1024,512]{1,0:T(8,128)(2,1)} collective-permute-done((bf16[1024,512]{1,0:T(8,128)(2,1)}, bf16[1024,512]{1,0:T(8,128)(2,1)}, u32[]{:S(2)}, u32[]{:S(2)}) %collective-permute-start.20) | collective-permute-done | bytes 1048608 | tf_op jit(solution)/shard_map/ppermute | solution.py:73
  122.1 2.6 %choose.3.refs_5_ = bf16[1024,512]{1,0:T(8,128)(2,1)} custom-call(s32[1]{0:T(128)} %bitcast.10.refs_0_, bf16[1024,512]{1,0:T(8,128)(2,1)} %collective-permute-done.20.refs_1_, bf16[1024,512]{1,0:T(8,128)(2,1)} %collective-permute-done.17.refs_0_.refs_2_, f32[512,512]{1,0:T(8,128)S(1)} %gram_inverse.1.refs_3_.refs_18_.refs_0_), custom_call_target="tpu_custom_call" | custom-call | flops 1 | bytes 1 | tf_op jit(solution)/shard_map/choose/pallas_call | solution.py:232
  129.3 5.2 %cross_add.4 = (f32[160,512]{1,0:T(8,128)S(1)}, f32[160,512]{1,0:T(8,128)S(1)}, f32[160,512]{1,0:T(8,128)S(1)}, f32[160,512]{1,0:T(8,128)S(1)}) custom-call(s32[6]{0:T(128)S(1)} %stack.143.index_ref, bf16[160,32768]{1,0:T(8,128)(2,1)} %refs_0_.7, bf16[8,160,1024]{2,1,0:T(8,128)(2,1)} %collective-permute-done.14.refs_7_.refs_1_.refs_13_, ...), custom_call_target="tpu_custom_call" | custom-call | flops 1 | bytes 1 | tf_op jit(solution)/shard_map/cross_add/pallas_call | solution.py:148
  134.5 4.3 %cross_add.5 = (f32[160,512]{1,0:T(8,128)S(1)}, f32[160,512]{1,0:T(8,128)S(1)}, f32[160,512]{1,0:T(8,128)S(1)}, f32[160,512]{1,0:T(8,128)S(1)}) custom-call(s32[4]{0:T(128)S(1)} %pad_add_fusion.6.index_ref, bf16[160,32768]{1,0:T(8,128)(2,1)} %refs_0_.7, ...), custom_call_target="tpu_custom_call", output_to_operand_aliasing={{0}: (13, {}), {1}: (14, {}), {2}: (15, {}), {3}: (16, {})} | custom-call | flops 1 | bytes 1 | tf_op jit(solution)/shard_map/cross_add/pallas_call | solution.py:148
  138.8 4.4 %cross_add.6 = (f32[160,512]{1,0:T(8,128)S(1)}, f32[160,512]{1,0:T(8,128)S(1)}, f32[160,512]{1,0:T(8,128)S(1)}, f32[160,512]{1,0:T(8,128)S(1)}) custom-call(s32[4]{0:T(128)S(1)} %pad_add_fusion.5.index_ref, bf16[160,32768]{1,0:T(8,128)(2,1)} %refs_0_.7, ...), custom_call_target="tpu_custom_call", output_to_operand_aliasing={{0}: (13, {}), {1}: (14, {}), {2}: (15, {}), {3}: (16, {})} | custom-call | flops 1 | bytes 1 | tf_op jit(solution)/shard_map/cross_add/pallas_call | solution.py:148
  143.2 3.0 %cross_add.7 = (f32[160,512]{1,0:T(8,128)S(1)}, f32[160,512]{1,0:T(8,128)S(1)}, f32[160,512]{1,0:T(8,128)S(1)}, f32[160,512]{1,0:T(8,128)S(1)}) custom-call(s32[2]{0:T(128)S(1)} %pad_add_fusion.4.index_ref, bf16[160,32768]{1,0:T(8,128)(2,1)} %refs_0_.7, ...), custom_call_target="tpu_custom_call", output_to_operand_aliasing={{0}: (7, {}), {1}: (8, {}), {2}: (9, {}), {3}: (10, {})} | custom-call | flops 1 | bytes 1 | tf_op jit(solution)/shard_map/cross_add/pallas_call | solution.py:148
  148.8 4.5 %collective-permute-done.25.refs_3_ = f32[160,512]{1,0:T(8,128)S(1)} collective-permute-done((f32[160,512]{1,0:T(8,128)S(1)}, f32[160,512]{1,0:T(8,128)S(1)}, u32[]{:S(2)}, u32[]{:S(2)}) %collective-permute-start.25) | collective-permute-done | bytes 327712 | tf_op jit(solution)/shard_map/ppermute | solution.py:73
  153.4 3.0 %collective-permute-done.26.refs_4_ = f32[160,512]{1,0:T(8,128)S(1)} collective-permute-done((f32[160,512]{1,0:T(8,128)S(1)}, f32[160,512]{1,0:T(8,128)S(1)}, u32[]{:S(2)}, u32[]{:S(2)}) %collective-permute-start.26) | collective-permute-done | bytes 327712 | tf_op jit(solution)/shard_map/ppermute | solution.py:73
  157.4 22.1 %all_to_all.19 = f32[16,32,160]{2,1,0:T(8,128)S(1)} all-to-all(f32[16,32,160]{2,1,0:T(8,128)S(1)} %bitcast.31), channel_id=1, replica_groups=mesh['donor'=16,'gene'=2] {'donor'}, dimensions={0} | all-to-all | bytes 655360 | tf_op jit(solution)/shard_map/all_to_all | solution.py:472
  (103 shorter events, 58.3 us)
Async XLA Ops:
  4.8 7.0 %collective-permute-start.1 = (f32[256,512]{1,0:T(8,128)S(1)}, f32[256,512]{1,0:T(8,128)S(1)}, u32[]{:S(2)}, u32[]{:S(2)}) collective-permute-start(f32[256,512]{1,0:T(8,128)S(1)} %gram_rows.2.refs_2_), channel_id=1, source_target_pairs={{0,1},{1,0},{2,3},{3,2},{4,5},{5,4},{6,7},{7,6},{8,9},{9,8},{10,11... | collective-permute-start | bytes 1572872 | tf_op jit(solution)/shard_map/ppermute | solution.py:73
  5.7 29.2 %collective-permute-start.4 = (bf16[1024,512]{1,0:T(8,128)(2,1)S(1)}, bf16[1024,512]{1,0:T(8,128)(2,1)}, u32[]{:S(2)}, u32[]{:S(2)}) collective-permute-start(bf16[1024,512]{1,0:T(8,128)(2,1)S(1)} %join_features.1.refs_1_.refs_5_), channel_id=1, source_target_pairs={{0,8},{1,9},{2,10},{3,11},{4,12},{5,13},{6,14},{7,15},{8,0},{9,1},... | collective-permute-start | bytes 3145736 | tf_op jit(solution)/shard_map/ppermute | solution.py:73
  8.5 26.4 %collective-permute-start.5 = (bf16[1024,512]{1,0:T(8,128)(2,1)S(1)}, bf16[1024,512]{1,0:T(8,128)(2,1)}, u32[]{:S(2)}, u32[]{:S(2)}) collective-permute-start(bf16[1024,512]{1,0:T(8,128)(2,1)S(1)} %join_features.1.refs_1_.refs_5_), channel_id=1, source_target_pairs={{8,16},{9,17},{10,18},{11,19},{12,20},{13,21},{14,22},{15,23},{16,... | collective-permute-start | bytes 3145736 | tf_op jit(solution)/shard_map/ppermute | solution.py:73
  10.2 24.8 %collective-permute-start.12 = (bf16[1024,512]{1,0:T(8,128)(2,1)S(1)}, bf16[1024,512]{1,0:T(8,128)(2,1)}, u32[]{:S(2)}, u32[]{:S(2)}) collective-permute-start(bf16[1024,512]{1,0:T(8,128)(2,1)S(1)} %join_features.1.refs_1_.refs_5_), channel_id=1, source_target_pairs={{0,4},{1,3},{2,6},{3,1},{4,0},{5,7},{6,2},{7,5},{8,12},{9,11},{10,... | collective-permute-start | bytes 3145736 | tf_op jit(solution)/shard_map/ppermute | solution.py:73
  18.7 48.1 %collective-permute-start.14 = (bf16[8,160,1024]{2,1,0:T(8,128)(2,1)}, bf16[8,160,1024]{2,1,0:T(8,128)(2,1)}, u32[]{:S(2)}, u32[]{:S(2)}) collective-permute-start(bf16[8,160,1024]{2,1,0:T(8,128)(2,1)} %pick_blocks.4.refs_3_), channel_id=1, source_target_pairs={{0,1},{1,0},{2,3},{3,2},{4,5},{5,4},{6,7},{7,6},{8,9},{9,8},{10,11... | collective-permute-start | bytes 7864328 | tf_op jit(solution)/shard_map/ppermute | solution.py:73
  18.7 8.2 %collective-permute-start.2 = (f32[128,512]{1,0:T(8,128)S(1)}, f32[128,512]{1,0:T(8,128)S(1)}, u32[]{:S(2)}, u32[]{:S(2)}) collective-permute-start(f32[128,512]{1,0:T(8,128)S(1)} %get-tuple-element.30), channel_id=1, source_target_pairs={{0,2},{1,5},{2,0},{3,7},{4,6},{5,1},{6,4},{7,3},{8,10},{9,13},{10,... | collective-permute-start | bytes 786440 | tf_op jit(solution)/shard_map/ppermute | solution.py:73
  29.8 5.2 %collective-permute-start.3 = (f32[64,512]{1,0:T(8,128)}, f32[64,512]{1,0:T(8,128)S(1)}, u32[]{:S(2)}, u32[]{:S(2)}) collective-permute-start(f32[64,512]{1,0:T(8,128)} %get-tuple-element.32), channel_id=1, source_target_pairs={{0,4},{1,3},{2,6},{3,1},{4,0},{5,7},{6,2},{7,5},{8,12},{9,11},{10,... | collective-permute-start | bytes 393224 | tf_op jit(solution)/shard_map/ppermute | solution.py:73
  37.9 28.8 %collective-permute-start.13 = (bf16[8,96,1024]{2,1,0:T(8,128)(2,1)}, bf16[8,96,1024]{2,1,0:T(8,128)(2,1)}, u32[]{:S(2)}, u32[]{:S(2)}) collective-permute-start(bf16[8,96,1024]{2,1,0:T(8,128)(2,1)} %pick_blocks.6), channel_id=1, source_target_pairs={{0,2},{1,5},{2,0},{3,7},{4,6},{5,1},{6,4},{7,3},{8,10},{9,13},{10,... | collective-permute-start | bytes 4718600 | tf_op jit(solution)/shard_map/ppermute | solution.py:73
  39.5 7.2 %collective-permute-start.6 = (f32[64,512]{1,0:T(8,128)S(1)}, f32[64,512]{1,0:T(8,128)S(1)}, u32[]{:S(2)}, u32[]{:S(2)}) collective-permute-start(f32[64,512]{1,0:T(8,128)S(1)} %add_all.2.refs_0_), channel_id=1, source_target_pairs={{0,8},{1,9},{2,10},{3,11},{4,12},{5,13},{6,14},{7,15},{8,0},{9,1},... | collective-permute-start | bytes 393224 | tf_op jit(solution)/shard_map/ppermute | solution.py:73
  42.8 11.7 %collective-permute-start.7 = (f32[64,512]{1,0:T(8,128)S(1)}, f32[64,512]{1,0:T(8,128)S(1)}, u32[]{:S(2)}, u32[]{:S(2)}) collective-permute-start(f32[64,512]{1,0:T(8,128)S(1)} %add_all.2.refs_0_), channel_id=1, source_target_pairs={{0,16},{1,17},{2,18},{3,19},{4,20},{5,21},{6,22},{7,23},{8,24},{9,... | collective-permute-start | bytes 393224 | tf_op jit(solution)/shard_map/ppermute | solution.py:73
  42.9 11.5 %collective-permute-start.8 = (f32[64,512]{1,0:T(8,128)S(1)}, f32[64,512]{1,0:T(8,128)S(1)}, u32[]{:S(2)}, u32[]{:S(2)}) collective-permute-start(f32[64,512]{1,0:T(8,128)S(1)} %add_all.2.refs_0_), channel_id=1, source_target_pairs={{0,24},{1,25},{2,26},{3,27},{4,28},{5,29},{6,30},{7,31},{8,16},{9,... | collective-permute-start | bytes 393224 | tf_op jit(solution)/shard_map/ppermute | solution.py:73
  54.4 7.5 %collective-permute-start.10 = (f32[64,512]{1,0:T(8,128)S(1)}, f32[64,512]{1,0:T(8,128)S(1)}, u32[]{:S(2)}, u32[]{:S(2)}) collective-permute-start(f32[64,512]{1,0:T(8,128)S(1)} %add_all.3.rest_0_.refs_1_), channel_id=1, source_target_pairs={{0,4},{1,5},{2,6},{3,7},{4,0},{5,1},{6,2},{7,3},{8,12},{9,13},{10,... | collective-permute-start | bytes 393224 | tf_op jit(solution)/shard_map/ppermute | solution.py:73
  55.5 8.3 %collective-permute-start.11 = (f32[64,512]{1,0:T(8,128)S(1)}, f32[64,512]{1,0:T(8,128)S(1)}, u32[]{:S(2)}, u32[]{:S(2)}) collective-permute-start(f32[64,512]{1,0:T(8,128)S(1)} %add_all.3.rest_0_.refs_1_), channel_id=1, source_target_pairs={{0,6},{1,7},{2,4},{3,5},{4,2},{5,3},{6,0},{7,1},{8,14},{9,15},{10,... | collective-permute-start | bytes 393224 | tf_op jit(solution)/shard_map/ppermute | solution.py:73
  57.5 7.6 %collective-permute-start.9 = (f32[64,512]{1,0:T(8,128)S(1)}, f32[64,512]{1,0:T(8,128)S(1)}, u32[]{:S(2)}, u32[]{:S(2)}) collective-permute-start(f32[64,512]{1,0:T(8,128)S(1)} %add_all.3.rest_0_.refs_1_), channel_id=1, source_target_pairs={{0,2},{1,3},{2,0},{3,1},{4,6},{5,7},{6,4},{7,5},{8,10},{9,11},{10,... | collective-permute-start | bytes 393224 | tf_op jit(solution)/shard_map/ppermute | solution.py:73
  61.9 27.3 %collective-permute-start.17 = (bf16[1024,512]{1,0:T(8,128)(2,1)}, bf16[1024,512]{1,0:T(8,128)(2,1)}, u32[]{:S(2)}, u32[]{:S(2)}) collective-permute-start(bf16[1024,512]{1,0:T(8,128)(2,1)} %collective-permute-done.4.refs_2_.rest_2_.refs_0_.refs_17_), channel_id=1, source_target_pairs={{8,16},{9,17},{10,18},{11,19},{12,20},{13,21},{14,22},{15,23},{16,... | collective-permute-start | bytes 3145736 | tf_op jit(solution)/shard_map/ppermute | solution.py:73
  63.8 28.7 %collective-permute-start.16 = (bf16[1024,512]{1,0:T(8,128)(2,1)}, bf16[1024,512]{1,0:T(8,128)(2,1)}, u32[]{:S(2)}, u32[]{:S(2)}) collective-permute-start(bf16[1024,512]{1,0:T(8,128)(2,1)} %collective-permute-done.5.refs_3_.rest_3_.refs_2_), channel_id=1, source_target_pairs={{8,0},{9,1},{10,2},{11,3},{12,4},{13,5},{14,6},{15,7},{16,24},{17,... | collective-permute-start | bytes 3145736 | tf_op jit(solution)/shard_map/ppermute | solution.py:73
  65.1 27.4 %collective-permute-start.18 = (bf16[8,64,1024]{2,1,0:T(8,128)(2,1)}, bf16[8,64,1024]{2,1,0:T(8,128)(2,1)}, u32[]{:S(2)}, u32[]{:S(2)}) collective-permute-start(bf16[8,64,1024]{2,1,0:T(8,128)(2,1)} %pick_blocks.5.refs_5_), channel_id=1, source_target_pairs={{0,2},{1,5},{2,0},{3,7},{4,6},{5,1},{6,4},{7,3},{8,10},{9,13},{10,... | collective-permute-start | bytes 3145736 | tf_op jit(solution)/shard_map/ppermute | solution.py:73
  73.6 53.2 %collective-permute-start.19 = (bf16[8,160,1024]{2,1,0:T(8,128)(2,1)}, bf16[8,160,1024]{2,1,0:T(8,128)(2,1)S(1)}, u32[]{:S(2)}, u32[]{:S(2)}) collective-permute-start(bf16[8,160,1024]{2,1,0:T(8,128)(2,1)} %pick_blocks.7.refs_3_), channel_id=1, source_target_pairs={{0,5},{1,2},{2,7},{3,0},{4,1},{5,6},{6,3},{7,4},{8,13},{9,10},{10,... | collective-permute-start | bytes 7864328 | tf_op jit(solution)/shard_map/ppermute | solution.py:73
  94.8 27.4 %collective-permute-start.20 = (bf16[1024,512]{1,0:T(8,128)(2,1)}, bf16[1024,512]{1,0:T(8,128)(2,1)}, u32[]{:S(2)}, u32[]{:S(2)}) collective-permute-start(bf16[1024,512]{1,0:T(8,128)(2,1)} %copy_rows.2.refs_1_), channel_id=1, source_target_pairs={{8,0},{9,1},{10,2},{11,3},{12,4},{13,5},{14,6},{15,7},{16,24},{17,... | collective-permute-start | bytes 3145736 | tf_op jit(solution)/shard_map/ppermute | solution.py:73
  98.6 35.9 %collective-permute-start.23 = (bf16[1024,512]{1,0:T(8,128)(2,1)}, bf16[1024,512]{1,0:T(8,128)(2,1)}, u32[]{:S(2)}, u32[]{:S(2)}) collective-permute-start(bf16[1024,512]{1,0:T(8,128)(2,1)} %copy_rows.3.refs_3_), channel_id=1, source_target_pairs={{0,4},{1,3},{2,6},{3,1},{4,0},{5,7},{6,2},{7,5},{8,12},{9,11},{10,... | collective-permute-start | bytes 3145736 | tf_op jit(solution)/shard_map/ppermute | solution.py:73
  102.5 36.2 %collective-permute-start.22 = (bf16[1024,512]{1,0:T(8,128)(2,1)}, bf16[1024,512]{1,0:T(8,128)(2,1)}, u32[]{:S(2)}, u32[]{:S(2)}) collective-permute-start(bf16[1024,512]{1,0:T(8,128)(2,1)} %choose.2.refs_1_.refs_5_), channel_id=1, source_target_pairs={{0,4},{1,3},{2,6},{3,1},{4,0},{5,7},{6,2},{7,5},{8,12},{9,11},{10,... | collective-permute-start | bytes 3145736 | tf_op jit(solution)/shard_map/ppermute | solution.py:73
  125.8 17.4 %collective-permute-start.21 = (bf16[1024,512]{1,0:T(8,128)(2,1)}, bf16[1024,512]{1,0:T(8,128)(2,1)}, u32[]{:S(2)}, u32[]{:S(2)}) collective-permute-start(bf16[1024,512]{1,0:T(8,128)(2,1)} %choose.3.refs_5_), channel_id=1, source_target_pairs={{0,4},{1,3},{2,6},{3,1},{4,0},{5,7},{6,2},{7,5},{8,12},{9,11},{10,... | collective-permute-start | bytes 3145736 | tf_op jit(solution)/shard_map/ppermute | solution.py:73
  146.2 7.1 %collective-permute-start.25 = (f32[160,512]{1,0:T(8,128)S(1)}, f32[160,512]{1,0:T(8,128)S(1)}, u32[]{:S(2)}, u32[]{:S(2)}) collective-permute-start(f32[160,512]{1,0:T(8,128)S(1)} %get-tuple-element.47), channel_id=1, source_target_pairs={{0,2},{1,5},{2,0},{3,7},{4,6},{5,1},{6,4},{7,3},{8,10},{9,13},{10,... | collective-permute-start | bytes 983048 | tf_op jit(solution)/shard_map/ppermute | solution.py:73
  147.8 8.5 %collective-permute-start.26 = (f32[160,512]{1,0:T(8,128)S(1)}, f32[160,512]{1,0:T(8,128)S(1)}, u32[]{:S(2)}, u32[]{:S(2)}) collective-permute-start(f32[160,512]{1,0:T(8,128)S(1)} %get-tuple-element.48), channel_id=1, source_target_pairs={{0,3},{1,4},{2,1},{3,6},{4,7},{5,0},{6,5},{7,2},{8,11},{9,12},{10,... | collective-permute-start | bytes 983048 | tf_op jit(solution)/shard_map/ppermute | solution.py:73
  (18 other events, 140.8 us)
